TPU v7x, 32 devices: a whole 2x2x4 slice. The times are simulated.
32 devices in a mesh: grp: 2 (over y), lat: 4 (over z), lay: 4 (over x, core).
Axes of the slice: x: 2, y: 2, z: 4, core: 2. Of those that a mesh axis runs over, the one named last changes fastest.
Arguments:
- acts: bfloat16 [128, 4, 1280], P(('grp', 'lat'), 'lay'), parts along dimension 0, may hold values from -6 to 6
- w_enc: bfloat16 [4, 1280, 1536], P('lay', None, 'lat'), may hold values from -0.078125 to 0.078125
- w_dec: bfloat16 [1536, 4, 1280], P('lat', 'lay'), may hold values from -0.15625 to 0.15625
- b_enc: float32 [1536], P('lat'), may hold values from -3 to 3
- b_dec: float32 [4, 1280], P('lay'), may hold values from -3 to 3
Outputs:
- lat_grad: bfloat16 [128, 1536], P('grp', 'lat'), parts along dimension 0
- enc_grad: bfloat16 [8, 1280, 1536], P(('grp', 'lay'), None, 'lat'), parts along dimension 0
- dec_grad: bfloat16 [1536, 8, 1280], P('lat', ('grp', 'lay')), parts along dimension 1
There are 2 independent parts, one for each index of `grp`. A program takes and returns all parts, laid end to end along the dimension named above; an argument that names none is the same for every part. Nothing has to cross between parts.
All inputs are finite; a program needn't handle non-finite values.
Results may differ from a plain program's by a relative error of at most 0.023.
Values may be sent and summed in bfloat16 or wider, within the bound.
No kernel may reach another device: no remote copies, remote signals or barrier semaphores. Data moves between devices by JAX's collectives and lax.ppermute only.
A program may use at most 64 MiB of HBM per device.

v0:
```python
import jax
import jax.numpy as jnp
from jax import lax
from jax.experimental import pallas as pl
from jax.experimental.pallas import tpu as pltpu
from jax.sharding import PartitionSpec as P


DIRECT = 4


def direct(size):
    return size <= DIRECT and size & (size - 1) == 0


def swap(x, axis, size, step):
    return lax.ppermute(x, axis, [(a, a ^ step) for a in range(size)])


def gather_blocks(x, axis, size):
    return [x] + [swap(x, axis, size, k) for k in range(1, size)]


def pair_sum(terms):
    while len(terms) > 1:
        terms = [terms[k] + terms[k + 1] for k in range(0, len(terms), 2)]
    return terms[0]


def all_sum(x, axis, size):
    if not direct(size):
        return lax.psum(x, axis).astype(jnp.float32)
    return pair_sum([t.astype(jnp.float32) for t in gather_blocks(x, axis, size)])


VMEM = pl.BlockSpec(memory_space=pltpu.VMEM)
HBM = pl.BlockSpec(memory_space=pltpu.HBM)
BLOCKS = 5
SMALL = pltpu.CompilerParams(vmem_limit_bytes=8 << 20)


def keep_near(*arrays):
    count = len(arrays)

    def kernel(*refs):
        sems = refs[-1]
        copies = [
            pltpu.make_async_copy(refs[n], refs[count + n], sems.at[n]) for n in range(count)
        ]
        for copy in copies:
            copy.start()
        for copy in copies:
            copy.wait()

    return pl.pallas_call(
        kernel,
        out_shape=[jax.ShapeDtypeStruct(a.shape, a.dtype) for a in arrays],
        in_specs=[HBM] * count,
        out_specs=[VMEM] * count,
        scratch_shapes=[pltpu.SemaphoreType.DMA((count,))],
        compiler_params=SMALL,
        name="keep_near",
    )(*[pltpu.with_memory_space_constraint(a, pltpu.HBM) for a in arrays])


def product(blocks, w):
    def kernel(*refs):
        *x_refs, w_ref, out_ref = refs
        x = jnp.concatenate([r[...] for r in x_refs], axis=0)
        out_ref[...] = jnp.dot(x, w_ref[...], preferred_element_type=jnp.float32).astype(out_ref.dtype)

    rows = sum(b.shape[0] for b in blocks)
    return pl.pallas_call(
        kernel,
        out_shape=jax.ShapeDtypeStruct((rows, w.shape[1]), jnp.bfloat16),
        in_specs=[VMEM] * (len(blocks) + 1),
        out_specs=VMEM,
        compiler_params=SMALL,
        name="product",
    )(*blocks, w)


def turned(blocks):
    def kernel(*refs):
        *x_refs, out_ref = refs
        out_ref[...] = jnp.concatenate([r[...] for r in x_refs], axis=0).T

    rows = sum(b.shape[0] for b in blocks)
    return pl.pallas_call(
        kernel,
        out_shape=jax.ShapeDtypeStruct((blocks[0].shape[1], rows), blocks[0].dtype),
        in_specs=[VMEM] * len(blocks),
        out_specs=VMEM,
        compiler_params=SMALL,
        name="turned",
    )(*blocks)


def last_stage(backs, slope, acts_t, lat):
    rows, lat_dev = slope.shape
    row_dev, depth = rows // lat, acts_t.shape[0]
    step = depth // BLOCKS
    count = len(backs)

    def kernel(*refs):
        b_refs, (slope_ref, x_ref, grad_ref, enc_ref, grad_held, held, sems) = (
            refs[:count],
            refs[count:],
        )
        total = pair_sum([r[...].astype(jnp.float32) for r in b_refs])
        grad = (total * slope_ref[...]).astype(jnp.bfloat16)
        me = lax.axis_index("lat")
        for k in range(lat):
            at = pl.multiple_of(lax.bitwise_xor(me, k) * row_dev, row_dev)
            grad_held[pl.ds(at, row_dev), :] = grad[k * row_dev : (k + 1) * row_dev]
        copies = [pltpu.make_async_copy(grad_held, grad_ref, sems.at[BLOCKS])]
        copies[0].start()
        for n in range(BLOCKS):
            part = pl.ds(n * step, step)
            held[part, :] = jnp.dot(
                x_ref[part, :], grad, preferred_element_type=jnp.float32
            ).astype(held.dtype)
            copies.append(pltpu.make_async_copy(held.at[part], enc_ref.at[part], sems.at[n]))
            copies[-1].start()
        for copy in copies:
            copy.wait()

    return pl.pallas_call(
        kernel,
        out_shape=(
            jax.ShapeDtypeStruct((rows, lat_dev), jnp.bfloat16),
            jax.ShapeDtypeStruct((depth, lat_dev), jnp.bfloat16),
        ),
        in_specs=[VMEM] * (count + 2),
        out_specs=(HBM, HBM),
        scratch_shapes=[
            pltpu.VMEM((rows, lat_dev), jnp.bfloat16),
            pltpu.VMEM((depth, lat_dev), jnp.bfloat16),
            pltpu.SemaphoreType.DMA((BLOCKS + 1,)),
        ],
        compiler_params=SMALL,
        name="last_stage",
    )(*backs, slope, acts_t)


def build(lat, lay):
    def step(acts, w_enc, w_dec, b_enc, b_dec):
        row_dev, lay_dev, width = acts.shape
        lat_dev = w_enc.shape[2]
        flat = lay_dev * width
        own = acts.reshape(row_dev, flat)
        we = w_enc.reshape(flat, lat_dev)
        wd = w_dec.reshape(lat_dev, flat)
        bd = b_dec.reshape(1, flat)
        near = direct(lat) and direct(lay)
        if near:
            blocks = gather_blocks(own, "lat", lat)
            blocks[0], we = keep_near(own, we)
            term = product(blocks, we)
            acts_t = turned(blocks)
            wd_t = turned([wd])
        else:
            gathered = lax.all_gather(own, "lat", axis=0, tiled=True)
            term = jnp.dot(gathered, we, preferred_element_type=jnp.float32)
        pre = all_sum(term.astype(jnp.bfloat16), "lay", lay) + b_enc[None, :]
        code = (jax.nn.softplus(4.0 * pre) / 4.0).astype(jnp.bfloat16)
        slope = jax.nn.sigmoid(4.0 * pre)
        part = jnp.dot(code, wd, preferred_element_type=jnp.float32).astype(jnp.bfloat16)
        if near:
            pieces = part.reshape(lat, row_dev, flat)
            mine = pair_sum(
                [pieces[0].astype(jnp.float32)]
                + [swap(pieces[k], "lat", lat, k).astype(jnp.float32) for k in range(1, lat)]
            )
        else:
            mine = lax.psum_scatter(part, "lat", scatter_dimension=0, tiled=True).astype(jnp.float32)
        err_own = (mine + bd - own.astype(jnp.float32)).astype(jnp.bfloat16)
        if near:
            errs = gather_blocks(err_own, "lat", lat)
            back = product(errs, wd_t)
            err = jnp.concatenate(errs, axis=0)
        else:
            err = lax.all_gather(err_own, "lat", axis=0, tiled=True)
            back = lax.dot_general(
                err, wd, (((1,), (1,)), ((), ())), preferred_element_type=jnp.float32
            ).astype(jnp.bfloat16)
        if near:
            lat_grad, enc_grad = last_stage(gather_blocks(back, "lay", lay), slope, acts_t, lat)
        else:
            lat_grad = (lax.psum(back, "lay").astype(jnp.float32) * slope).astype(jnp.bfloat16)
            enc_grad = lax.dot_general(
                gathered, lat_grad, (((0,), (0,)), ((), ())), preferred_element_type=jnp.float32
            ).astype(jnp.bfloat16)
        dec_grad = lax.dot_general(
            code, err, (((0,), (0,)), ((), ())), preferred_element_type=jnp.float32
        ).astype(jnp.bfloat16)
        return (
            lat_grad,
            enc_grad.reshape(lay_dev, width, lat_dev),
            dec_grad.reshape(lat_dev, lay_dev, width),
        )

    return step


def solution(mesh):
    in_specs = (
        P(("grp", "lat"), "lay", None),
        P("lay", None, "lat"),
        P("lat", "lay", None),
        P("lat"),
        P("lay", None),
    )
    out_specs = (P("grp", "lat"), P(("grp", "lay"), None, "lat"), P("lat", ("grp", "lay"), None))
    lat, lay = mesh.shape["lat"], mesh.shape["lay"]
    return jax.shard_map(
        build(lat, lay), mesh=mesh, in_specs=in_specs, out_specs=out_specs, check_vma=False
    )
```

profile of v0, /device:TPU:0, one launch (start us, length us, event | category | flops | bytes accessed | tf_op | source)
XLA Modules:
  0.0 38.2 jit_solution(12045716022216969368)
XLA Ops:
  0.6 5.1 %collective-permute-start.2 = (bf16[16,1280]{1,0:T(8,128)(2,1)}, bf16[16,1280]{1,0:T(8,128)(2,1)S(1)}, u32[]{:S(2)}, u32[]{:S(2)}) collective-permute-start(bf16[16,1280]{1,0:T(8,128)(2,1)} %bitcast.13), channel_id=1, source_target_pairs={{0,12},{4,8},{8,4},{12,0},{1,13},{5,9},{9,5},{13,1},{2,14},{6,10},... | collective-permute-start | bytes 122888 | tf_op jit(solution)/shard_map/ppermute | solution.py:17
  5.8 0.0 collective-permute-start.1
  5.8 0.6 %collective-permute-start = (bf16[16,1280]{1,0:T(8,128)(2,1)}, bf16[16,1280]{1,0:T(8,128)(2,1)S(1)}, u32[]{:S(2)}, u32[]{:S(2)}) collective-permute-start(bf16[16,1280]{1,0:T(8,128)(2,1)} %bitcast.15), channel_id=1, source_target_pairs={{0,4},{4,0},{8,12},{12,8},{1,5},{5,1},{9,13},{13,9},{2,6},{6,2},{1... | collective-permute-start | bytes 122888 | tf_op jit(solution)/shard_map/ppermute | solution.py:17
  6.4 0.0 copy-start.3
  6.4 1.3 %keep_near.1 = (bf16[16,1280]{1,0:T(8,128)(2,1)S(1)}, bf16[1280,384]{1,0:T(8,128)(2,1)S(1)}) custom-call(bf16[16,1280]{1,0:T(8,128)(2,1)} %bitcast.16, bf16[1280,384]{1,0:T(8,128)(2,1)} %bitcast.12), custom_call_target="tpu_custom_call" | custom-call | tf_op jit(solution)/shard_map/keep_near/pallas_call | solution.py:55
  7.7 0.0 copy-start
  7.7 0.3 collective-permute-done.2.refs_3_
  8.0 2.9 %collective-permute-done.1.refs_2_ = bf16[16,1280]{1,0:T(8,128)(2,1)S(1)} collective-permute-done((bf16[16,1280]{1,0:T(8,128)(2,1)}, bf16[16,1280]{1,0:T(8,128)(2,1)S(1)}, u32[]{:S(2)}, u32[]{:S(2)}) %collective-permute-start.1) | collective-permute-done | bytes 40992 | tf_op jit(solution)/shard_map/ppermute | solution.py:17
  10.9 0.0 collective-permute-done.refs_1_
  10.9 0.3 product.2
  11.2 0.0 copy-start.2
  11.2 0.0 copy-start.1
  11.2 0.1 collective-permute-start.5
  11.3 1.6 %collective-permute-start.4 = (bf16[64,384]{1,0:T(8,128)(2,1)S(1)}, bf16[64,384]{1,0:T(8,128)(2,1)S(1)}, u32[]{:S(2)}, u32[]{:S(2)}) collective-permute-start(bf16[64,384]{1,0:T(8,128)(2,1)S(1)} %product.2), channel_id=1, source_target_pairs={{0,2},{1,3},{2,0},{3,1},{4,6},{5,7},{6,4},{7,5},{8,10},{9,11},{10,... | collective-permute-start | bytes 147464 | tf_op jit(solution)/shard_map/ppermute | solution.py:17
  12.8 0.3 collective-permute-start.3
  13.1 2.1 %collective-permute-done.5 = bf16[64,384]{1,0:T(8,128)(2,1)S(1)} collective-permute-done((bf16[64,384]{1,0:T(8,128)(2,1)S(1)}, bf16[64,384]{1,0:T(8,128)(2,1)S(1)}, u32[]{:S(2)}, u32[]{:S(2)}) %collective-permute-start.5) | collective-permute-done | bytes 49184 | tf_op jit(solution)/shard_map/ppermute | solution.py:17
  15.3 0.9 %collective-permute-done.4 = bf16[64,384]{1,0:T(8,128)(2,1)S(1)} collective-permute-done((bf16[64,384]{1,0:T(8,128)(2,1)S(1)}, bf16[64,384]{1,0:T(8,128)(2,1)S(1)}, u32[]{:S(2)}, u32[]{:S(2)}) %collective-permute-start.4) | collective-permute-done | bytes 49184 | tf_op jit(solution)/shard_map/ppermute | solution.py:17
  16.2 0.0 collective-permute-done.3
  16.2 0.0 copy-done.3
  16.2 0.1 add_divide_fusion
  16.3 0.0 copy-done
  16.3 0.3 convolution_convert_fusion.1
  16.6 0.2 collective-permute-start.6
  16.8 3.3 %collective-permute-start.8 = (bf16[16,1280]{1,0:T(8,128)(2,1)S(1)}, bf16[16,1280]{1,0:T(8,128)(2,1)S(1)}, u32[]{:S(2)}, u32[]{:S(2)}) collective-permute-start(bf16[16,1280]{1,0:T(8,128)(2,1)S(1)} %get-tuple-element.14), channel_id=1, source_target_pairs={{0,12},{4,8},{8,4},{12,0},{1,13},{5,9},{9,5},{13,1},{2,14},{6,10},... | collective-permute-start | bytes 122888 | tf_op jit(solution)/shard_map/ppermute | solution.py:17
  20.2 0.0 collective-permute-start.7
  20.2 0.0 copy-done.2
  20.2 0.5 %collective-permute-done.6 = bf16[16,1280]{1,0:T(8,128)(2,1)S(1)} collective-permute-done((bf16[16,1280]{1,0:T(8,128)(2,1)S(1)}, bf16[16,1280]{1,0:T(8,128)(2,1)S(1)}, u32[]{:S(2)}, u32[]{:S(2)}) %collective-permute-start.6) | collective-permute-done | bytes 40992 | tf_op jit(solution)/shard_map/ppermute | solution.py:17
  20.7 2.4 %collective-permute-done.8 = bf16[16,1280]{1,0:T(8,128)(2,1)S(1)} collective-permute-done((bf16[16,1280]{1,0:T(8,128)(2,1)S(1)}, bf16[16,1280]{1,0:T(8,128)(2,1)S(1)}, u32[]{:S(2)}, u32[]{:S(2)}) %collective-permute-start.8) | collective-permute-done | bytes 40992 | tf_op jit(solution)/shard_map/ppermute | solution.py:17
  23.1 2.0 %collective-permute-done.7 = bf16[16,1280]{1,0:T(8,128)(2,1)S(1)} collective-permute-done((bf16[16,1280]{1,0:T(8,128)(2,1)S(1)}, bf16[16,1280]{1,0:T(8,128)(2,1)S(1)}, u32[]{:S(2)}, u32[]{:S(2)}) %collective-permute-start.7) | collective-permute-done | bytes 40992 | tf_op jit(solution)/shard_map/ppermute | solution.py:17
  25.1 0.0 copy-done.1
  25.1 1.6 %collective-permute-start.11 = (bf16[16,1280]{1,0:T(8,128)(2,1)S(1)}, bf16[16,1280]{1,0:T(8,128)(2,1)S(1)}, u32[]{:S(2)}, u32[]{:S(2)}) collective-permute-start(bf16[16,1280]{1,0:T(8,128)(2,1)S(1)} %subtract_convert_fusion.refs_0_), channel_id=1, source_target_pairs={{0,12},{4,8},{8,4},{12,0},{1,13},{5,9},{9,5},{13,1},{2,14},{6,10},... | collective-permute-start | bytes 122888 | tf_op jit(solution)/shard_map/ppermute | solution.py:17
  26.7 0.0 collective-permute-start.10
  26.7 2.9 %collective-permute-start.9 = (bf16[16,1280]{1,0:T(8,128)(2,1)S(1)}, bf16[16,1280]{1,0:T(8,128)(2,1)S(1)}, u32[]{:S(2)}, u32[]{:S(2)}) collective-permute-start(bf16[16,1280]{1,0:T(8,128)(2,1)S(1)} %subtract_convert_fusion.refs_0_), channel_id=1, source_target_pairs={{0,4},{4,0},{8,12},{12,8},{1,5},{5,1},{9,13},{13,9},{2,6},{6,2},{1... | collective-permute-start | bytes 122888 | tf_op jit(solution)/shard_map/ppermute | solution.py:17
  29.6 0.3 turned.2.refs_4_
  29.9 0.1 turned.3.refs_5_
  30.0 1.0 %collective-permute-done.11.refs_3_ = bf16[16,1280]{1,0:T(8,128)(2,1)S(1)} collective-permute-done((bf16[16,1280]{1,0:T(8,128)(2,1)S(1)}, bf16[16,1280]{1,0:T(8,128)(2,1)S(1)}, u32[]{:S(2)}, u32[]{:S(2)}) %collective-permute-start.11) | collective-permute-done | bytes 40992 | tf_op jit(solution)/shard_map/ppermute | solution.py:17
  31.0 1.0 %collective-permute-done.10.refs_2_ = bf16[16,1280]{1,0:T(8,128)(2,1)S(1)} collective-permute-done((bf16[16,1280]{1,0:T(8,128)(2,1)S(1)}, bf16[16,1280]{1,0:T(8,128)(2,1)S(1)}, u32[]{:S(2)}, u32[]{:S(2)}) %collective-permute-start.10) | collective-permute-done | bytes 40992 | tf_op jit(solution)/shard_map/ppermute | solution.py:17
  32.0 0.0 collective-permute-done.9.refs_1_
  32.0 0.3 product.3.refs_0_
  32.3 0.1 collective-permute-start.14
  32.4 1.2 %collective-permute-start.13 = (bf16[64,384]{1,0:T(8,128)(2,1)S(1)}, bf16[64,384]{1,0:T(8,128)(2,1)S(1)}, u32[]{:S(2)}, u32[]{:S(2)}) collective-permute-start(bf16[64,384]{1,0:T(8,128)(2,1)S(1)} %product.3.refs_0_), channel_id=1, source_target_pairs={{0,2},{1,3},{2,0},{3,1},{4,6},{5,7},{6,4},{7,5},{8,10},{9,11},{10,... | collective-permute-start | bytes 147464 | tf_op jit(solution)/shard_map/ppermute | solution.py:17
  33.5 0.7 %collective-permute-start.12 = (bf16[64,384]{1,0:T(8,128)(2,1)S(1)}, bf16[64,384]{1,0:T(8,128)(2,1)S(1)}, u32[]{:S(2)}, u32[]{:S(2)}) collective-permute-start(bf16[64,384]{1,0:T(8,128)(2,1)S(1)} %product.3.refs_0_), channel_id=1, source_target_pairs={{0,1},{1,0},{2,3},{3,2},{4,5},{5,4},{6,7},{7,6},{8,9},{9,8},{10,11... | collective-permute-start | bytes 147464 | tf_op jit(solution)/shard_map/ppermute | solution.py:17
  34.2 1.4 %fusion = bf16[384,1,1280]{2,0,1:T(8,128)(2,1)} fusion(bf16[64,384]{1,0:T(8,128)(2,1)S(1)} %get-tuple-element.12, bf16[16,1280]{1,0:T(8,128)(2,1)S(1)} %collective-permute-done.11.refs_3_, bf16[16,1280]{1,0:T(8,128)(2,1)S(1)} %collective-permute-done.10.refs_2_, bf16[16,1280]{1,0:T(8,128)(2,1)S(1)} %collective-permute-done.9.refs_1_, ...), kind=kOutput, calls=%fused_computation.1 | convolution fusion | flops 64061440 | bytes 1196032 | tf_op jit(solution)/shard_map/dot_general | solution.py:194
  35.6 0.5 %collective-permute-done.14.refs_3_ = bf16[64,384]{1,0:T(8,128)(2,1)S(1)} collective-permute-done((bf16[64,384]{1,0:T(8,128)(2,1)S(1)}, bf16[64,384]{1,0:T(8,128)(2,1)S(1)}, u32[]{:S(2)}, u32[]{:S(2)}) %collective-permute-start.14) | collective-permute-done | bytes 49184 | tf_op jit(solution)/shard_map/ppermute | solution.py:17
  36.1 0.9 %collective-permute-done.13.refs_2_ = bf16[64,384]{1,0:T(8,128)(2,1)S(1)} collective-permute-done((bf16[64,384]{1,0:T(8,128)(2,1)S(1)}, bf16[64,384]{1,0:T(8,128)(2,1)S(1)}, u32[]{:S(2)}, u32[]{:S(2)}) %collective-permute-start.13) | collective-permute-done | bytes 49184 | tf_op jit(solution)/shard_map/ppermute | solution.py:17
  37.0 0.0 collective-permute-done.12.refs_1_
  37.0 1.2 %last_stage.1 = (bf16[64,384]{1,0:T(8,128)(2,1)}, bf16[1280,384]{1,0:T(8,128)(2,1)}) custom-call(bf16[64,384]{1,0:T(8,128)(2,1)S(1)} %product.3.refs_0_, bf16[64,384]{1,0:T(8,128)(2,1)S(1)} %collective-permute-done.12.refs_1_, bf16[64,384]{1,0:T(8,128)(2,1)S(1)} %collective-permute-done.13.refs_2_, bf16[64,384]{1,0:T(8,128)(2,1)S(1)} %collective-permute-done.14.refs_3_, ...), custom_call_target="tpu_custom_call" | custom-call | tf_op jit(solution)/shard_map/last_stage/pallas_call | solution.py:128
  (3 shorter events, 0.1 us)
Async XLA Ops:
  0.6 7.3 %collective-permute-start.2 = (bf16[16,1280]{1,0:T(8,128)(2,1)}, bf16[16,1280]{1,0:T(8,128)(2,1)S(1)}, u32[]{:S(2)}, u32[]{:S(2)}) collective-permute-start(bf16[16,1280]{1,0:T(8,128)(2,1)} %bitcast.13), channel_id=1, source_target_pairs={{0,12},{4,8},{8,4},{12,0},{1,13},{5,9},{9,5},{13,1},{2,14},{6,10},... | collective-permute-start | bytes 122888 | tf_op jit(solution)/shard_map/ppermute | solution.py:17
  5.8 5.1 %collective-permute-start.1 = (bf16[16,1280]{1,0:T(8,128)(2,1)}, bf16[16,1280]{1,0:T(8,128)(2,1)S(1)}, u32[]{:S(2)}, u32[]{:S(2)}) collective-permute-start(bf16[16,1280]{1,0:T(8,128)(2,1)} %bitcast.14), channel_id=1, source_target_pairs={{0,8},{4,12},{8,0},{12,4},{1,9},{5,13},{9,1},{13,5},{2,10},{6,14},... | collective-permute-start | bytes 122888 | tf_op jit(solution)/shard_map/ppermute | solution.py:17
  5.8 5.1 %collective-permute-start = (bf16[16,1280]{1,0:T(8,128)(2,1)}, bf16[16,1280]{1,0:T(8,128)(2,1)S(1)}, u32[]{:S(2)}, u32[]{:S(2)}) collective-permute-start(bf16[16,1280]{1,0:T(8,128)(2,1)} %bitcast.15), channel_id=1, source_target_pairs={{0,4},{4,0},{8,12},{12,8},{1,5},{5,1},{9,13},{13,9},{2,6},{6,2},{1... | collective-permute-start | bytes 122888 | tf_op jit(solution)/shard_map/ppermute | solution.py:17
  6.4 9.8 %copy-start.3 = (f32[384]{0:T(512)S(1)}, f32[384]{0:T(512)}, u32[]{:S(2)}) copy-start(f32[384]{0:T(512)} %param.8) | copy-start | bytes 4612
  7.7 8.6 %copy-start = (bf16[384,1,1280]{2,0,1:T(8,128)(2,1)S(1)}, bf16[384,1,1280]{2,0,1:T(8,128)(2,1)}, u32[]{:S(2)}) copy-start(bf16[384,1,1280]{2,0,1:T(8,128)(2,1)} %param.7) | copy-start | bytes 2949124
  11.2 9.0 %copy-start.2 = (f32[1,1280]{1,0:T(1,128)S(1)}, f32[1,1280]{1,0:T(1,128)}, u32[]{:S(2)}) copy-start(f32[1,1280]{1,0:T(1,128)} %param.9) | copy-start | bytes 15364
  11.2 13.9 %copy-start.1 = (bf16[16,1,1280]{2,0,1:T(8,128)(2,1)S(1)}, bf16[16,1,1280]{2,0,1:T(8,128)(2,1)}, u32[]{:S(2)}) copy-start(bf16[16,1,1280]{2,0,1:T(8,128)(2,1)} %param.5) | copy-start | bytes 122884
  11.2 4.1 %collective-permute-start.5 = (bf16[64,384]{1,0:T(8,128)(2,1)S(1)}, bf16[64,384]{1,0:T(8,128)(2,1)S(1)}, u32[]{:S(2)}, u32[]{:S(2)}) collective-permute-start(bf16[64,384]{1,0:T(8,128)(2,1)S(1)} %product.2), channel_id=1, source_target_pairs={{0,3},{1,2},{2,1},{3,0},{4,7},{5,6},{6,5},{7,4},{8,11},{9,10},{10,... | collective-permute-start | bytes 147464 | tf_op jit(solution)/shard_map/ppermute | solution.py:17
  11.3 4.9 %collective-permute-start.4 = (bf16[64,384]{1,0:T(8,128)(2,1)S(1)}, bf16[64,384]{1,0:T(8,128)(2,1)S(1)}, u32[]{:S(2)}, u32[]{:S(2)}) collective-permute-start(bf16[64,384]{1,0:T(8,128)(2,1)S(1)} %product.2), channel_id=1, source_target_pairs={{0,2},{1,3},{2,0},{3,1},{4,6},{5,7},{6,4},{7,5},{8,10},{9,11},{10,... | collective-permute-start | bytes 147464 | tf_op jit(solution)/shard_map/ppermute | solution.py:17
  12.8 3.4 %collective-permute-start.3 = (bf16[64,384]{1,0:T(8,128)(2,1)S(1)}, bf16[64,384]{1,0:T(8,128)(2,1)S(1)}, u32[]{:S(2)}, u32[]{:S(2)}) collective-permute-start(bf16[64,384]{1,0:T(8,128)(2,1)S(1)} %product.2), channel_id=1, source_target_pairs={{0,1},{1,0},{2,3},{3,2},{4,5},{5,4},{6,7},{7,6},{8,9},{9,8},{10,11... | collective-permute-start | bytes 147464 | tf_op jit(solution)/shard_map/ppermute | solution.py:17
  16.6 4.1 %collective-permute-start.6 = (bf16[16,1280]{1,0:T(8,128)(2,1)S(1)}, bf16[16,1280]{1,0:T(8,128)(2,1)S(1)}, u32[]{:S(2)}, u32[]{:S(2)}) collective-permute-start(bf16[16,1280]{1,0:T(8,128)(2,1)S(1)} %get-tuple-element.13), channel_id=1, source_target_pairs={{0,4},{4,0},{8,12},{12,8},{1,5},{5,1},{9,13},{13,9},{2,6},{6,2},{1... | collective-permute-start | bytes 122888 | tf_op jit(solution)/shard_map/ppermute | solution.py:17
  16.8 6.2 %collective-permute-start.8 = (bf16[16,1280]{1,0:T(8,128)(2,1)S(1)}, bf16[16,1280]{1,0:T(8,128)(2,1)S(1)}, u32[]{:S(2)}, u32[]{:S(2)}) collective-permute-start(bf16[16,1280]{1,0:T(8,128)(2,1)S(1)} %get-tuple-element.14), channel_id=1, source_target_pairs={{0,12},{4,8},{8,4},{12,0},{1,13},{5,9},{9,5},{13,1},{2,14},{6,10},... | collective-permute-start | bytes 122888 | tf_op jit(solution)/shard_map/ppermute | solution.py:17
  20.2 4.9 %collective-permute-start.7 = (bf16[16,1280]{1,0:T(8,128)(2,1)S(1)}, bf16[16,1280]{1,0:T(8,128)(2,1)S(1)}, u32[]{:S(2)}, u32[]{:S(2)}) collective-permute-start(bf16[16,1280]{1,0:T(8,128)(2,1)S(1)} %get-tuple-element.15), channel_id=1, source_target_pairs={{0,8},{4,12},{8,0},{12,4},{1,9},{5,13},{9,1},{13,5},{2,10},{6,14},... | collective-permute-start | bytes 122888 | tf_op jit(solution)/shard_map/ppermute | solution.py:17
  25.1 5.9 %collective-permute-start.11 = (bf16[16,1280]{1,0:T(8,128)(2,1)S(1)}, bf16[16,1280]{1,0:T(8,128)(2,1)S(1)}, u32[]{:S(2)}, u32[]{:S(2)}) collective-permute-start(bf16[16,1280]{1,0:T(8,128)(2,1)S(1)} %subtract_convert_fusion.refs_0_), channel_id=1, source_target_pairs={{0,12},{4,8},{8,4},{12,0},{1,13},{5,9},{9,5},{13,1},{2,14},{6,10},... | collective-permute-start | bytes 122888 | tf_op jit(solution)/shard_map/ppermute | solution.py:17
  26.7 5.3 %collective-permute-start.10 = (bf16[16,1280]{1,0:T(8,128)(2,1)S(1)}, bf16[16,1280]{1,0:T(8,128)(2,1)S(1)}, u32[]{:S(2)}, u32[]{:S(2)}) collective-permute-start(bf16[16,1280]{1,0:T(8,128)(2,1)S(1)} %subtract_convert_fusion.refs_0_), channel_id=1, source_target_pairs={{0,8},{4,12},{8,0},{12,4},{1,9},{5,13},{9,1},{13,5},{2,10},{6,14},... | collective-permute-start | bytes 122888 | tf_op jit(solution)/shard_map/ppermute | solution.py:17
  26.7 5.3 %collective-permute-start.9 = (bf16[16,1280]{1,0:T(8,128)(2,1)S(1)}, bf16[16,1280]{1,0:T(8,128)(2,1)S(1)}, u32[]{:S(2)}, u32[]{:S(2)}) collective-permute-start(bf16[16,1280]{1,0:T(8,128)(2,1)S(1)} %subtract_convert_fusion.refs_0_), channel_id=1, source_target_pairs={{0,4},{4,0},{8,12},{12,8},{1,5},{5,1},{9,13},{13,9},{2,6},{6,2},{1... | collective-permute-start | bytes 122888 | tf_op jit(solution)/shard_map/ppermute | solution.py:17
  32.3 3.8 %collective-permute-start.14 = (bf16[64,384]{1,0:T(8,128)(2,1)S(1)}, bf16[64,384]{1,0:T(8,128)(2,1)S(1)}, u32[]{:S(2)}, u32[]{:S(2)}) collective-permute-start(bf16[64,384]{1,0:T(8,128)(2,1)S(1)} %product.3.refs_0_), channel_id=1, source_target_pairs={{0,3},{1,2},{2,1},{3,0},{4,7},{5,6},{6,5},{7,4},{8,11},{9,10},{10,... | collective-permute-start | bytes 147464 | tf_op jit(solution)/shard_map/ppermute | solution.py:17
  32.4 4.6 %collective-permute-start.13 = (bf16[64,384]{1,0:T(8,128)(2,1)S(1)}, bf16[64,384]{1,0:T(8,128)(2,1)S(1)}, u32[]{:S(2)}, u32[]{:S(2)}) collective-permute-start(bf16[64,384]{1,0:T(8,128)(2,1)S(1)} %product.3.refs_0_), channel_id=1, source_target_pairs={{0,2},{1,3},{2,0},{3,1},{4,6},{5,7},{6,4},{7,5},{8,10},{9,11},{10,... | collective-permute-start | bytes 147464 | tf_op jit(solution)/shard_map/ppermute | solution.py:17
  33.5 3.5 %collective-permute-start.12 = (bf16[64,384]{1,0:T(8,128)(2,1)S(1)}, bf16[64,384]{1,0:T(8,128)(2,1)S(1)}, u32[]{:S(2)}, u32[]{:S(2)}) collective-permute-start(bf16[64,384]{1,0:T(8,128)(2,1)S(1)} %product.3.refs_0_), channel_id=1, source_target_pairs={{0,1},{1,0},{2,3},{3,2},{4,5},{5,4},{6,7},{7,6},{8,9},{9,8},{10,11... | collective-permute-start | bytes 147464 | tf_op jit(solution)/shard_map/ppermute | solution.py:17
where the time goes:
time: 38.3 us; the launch traced here: 38.2 us
  starting transfers between devices  17.6 us (46%)
  waiting for transfers between devices  14.5 us (38%)
  Pallas kernels  3.46 us (9%)
  matrix products  1.66 us (4%)
  between operations  0.75 us (2%)
    ppermute x15, starting transfers between devices, swap(): return lax.ppermute(x, axis, [(a, a ^ step) for a in range(size)])  17.6 us
    ppermute x15, waiting for transfers between devices, swap(): return lax.ppermute(x, axis, [(a, a ^ step) for a in range(size)])  14.5 us
    dot_general x1, matrix products, step(): lax.dot_general(code, err, (((0,), (0,)), ((), ())), preferred_element_ty...  1.39 us
    pallas_call x1, Pallas kernels, keep_near(): pl.pallas_call(kernel, out_shape=[jax.ShapeDtypeStruct(a.shape, a.dtype)...  1.26 us
    pallas_call x1, Pallas kernels, last_stage(): pl.pallas_call(kernel, out_shape=(jax.ShapeDtypeStruct((rows, lat_dev), j...  1.2 us
  transfers between devices with their start and end apart: 15, of which 11 were waited for; matrix products, arithmetic and copies ran while one was open for 4% of the time, Pallas kernels for 4%

commit v1 on v0

--- a/solution.py
+++ b/solution.py
@@ -10,7 +10,7 @@
 
 
 def direct(size):
-    return size <= DIRECT and size & (size - 1) == 0
+    return 2 <= size <= DIRECT and size & (size - 1) == 0
 
 
 def swap(x, axis, size, step):
@@ -19,18 +19,19 @@
 
 def gather_blocks(x, axis, size):
     return [x] + [swap(x, axis, size, k) for k in range(1, size)]
+
+
+def cross(x, lat, lay, step):
+    pairs = [
+        (a * lay + b, (a ^ step) * lay + (b ^ 1)) for a in range(lat) for b in range(lay)
+    ]
+    return lax.ppermute(x, ("lat", "lay"), pairs)
 
 
 def pair_sum(terms):
     while len(terms) > 1:
         terms = [terms[k] + terms[k + 1] for k in range(0, len(terms), 2)]
     return terms[0]
-
-
-def all_sum(x, axis, size):
-    if not direct(size):
-        return lax.psum(x, axis).astype(jnp.float32)
-    return pair_sum([t.astype(jnp.float32) for t in gather_blocks(x, axis, size)])
 
 
 VMEM = pl.BlockSpec(memory_space=pltpu.VMEM)
@@ -94,6 +95,44 @@
         compiler_params=SMALL,
         name="turned",
     )(*blocks)
+
+
+def recon_pieces(terms, b_enc, wd, own, b_dec):
+    count, (rows, lat_dev), (row_dev, width) = len(terms), terms[0].shape, own.shape
+
+    def kernel(*refs):
+        t_refs, (b_enc_ref, wd_ref, own_ref, b_dec_ref, code_ref, slope_ref), piece_refs = (
+            refs[:count],
+            refs[count : count + 6],
+            refs[count + 6 :],
+        )
+        pre = pair_sum([r[...].astype(jnp.float32) for r in t_refs]) + b_enc_ref[...]
+        x = 4.0 * pre
+        soft = jnp.maximum(x, 0.0) + jnp.log1p(jnp.exp(-jnp.abs(x)))
+        code = (soft * 0.25).astype(jnp.bfloat16)
+        code_ref[...] = code
+        slope_ref[...] = jax.nn.sigmoid(x)
+        part = jnp.dot(code, wd_ref[...], preferred_element_type=jnp.float32)
+        for k, ref in enumerate(piece_refs):
+            piece = part[k * row_dev : (k + 1) * row_dev]
+            if k == 0:
+                piece = piece + b_dec_ref[...] - own_ref[...].astype(jnp.float32)
+            ref[...] = piece.astype(jnp.bfloat16)
+
+    pieces = rows // row_dev
+    code, slope, *parts = pl.pallas_call(
+        kernel,
+        out_shape=[
+            jax.ShapeDtypeStruct((rows, lat_dev), jnp.bfloat16),
+            jax.ShapeDtypeStruct((rows, lat_dev), jnp.float32),
+        ]
+        + [jax.ShapeDtypeStruct((row_dev, width), jnp.bfloat16)] * pieces,
+        in_specs=[VMEM] * (count + 4),
+        out_specs=[VMEM] * (2 + pieces),
+        compiler_params=SMALL,
+        name="recon_pieces",
+    )(*terms, b_enc, wd, own, b_dec)
+    return code, slope, parts
 
 
 def last_stage(backs, slope, acts_t, lat):
@@ -143,54 +182,56 @@
     )(*backs, slope, acts_t)
 
 
-def build(lat, lay):
-    def step(acts, w_enc, w_dec, b_enc, b_dec):
+def near_step(lat, lay):
+    def step(own, we, wd, b_enc, b_dec):
+        blocks = gather_blocks(own, "lat", lat)
+        blocks[0], we = keep_near(own, we)
+        terms = gather_blocks(product(blocks, we), "lay", lay)
+        acts_t = turned(blocks)
+        code, slope, parts = recon_pieces(terms, b_enc, wd, blocks[0], b_dec)
+        err_own = pair_sum(
+            [cross(p, lat, lay, k).astype(jnp.float32) for k, p in enumerate(parts)]
+        ).astype(jnp.bfloat16)
+        wd_t = turned([wd])
+        errs = [cross(err_own, lat, lay, k) for k in range(lat)]
+        backs = gather_blocks(product(errs, wd_t), "lay", lay)
+        lat_grad, enc_grad = last_stage(backs, slope, acts_t, lat)
+        return lat_grad, enc_grad, code, jnp.concatenate(errs, axis=0)
+
+    return step
+
+
+def far_step(own, we, wd, b_enc, b_dec):
+    gathered = lax.all_gather(own, "lat", axis=0, tiled=True)
+    term = jnp.dot(gathered, we, preferred_element_type=jnp.float32)
+    pre = lax.psum(term.astype(jnp.bfloat16), "lay").astype(jnp.float32) + b_enc
+    code = (jax.nn.softplus(4.0 * pre) / 4.0).astype(jnp.bfloat16)
+    slope = jax.nn.sigmoid(4.0 * pre)
+    part = jnp.dot(code, wd, preferred_element_type=jnp.float32).astype(jnp.bfloat16)
+    mine = lax.psum_scatter(part, "lat", scatter_dimension=0, tiled=True).astype(jnp.float32)
+    err_own = (mine + b_dec - own.astype(jnp.float32)).astype(jnp.bfloat16)
+    err = lax.all_gather(err_own, "lat", axis=0, tiled=True)
+    back = lax.dot_general(err, wd, (((1,), (1,)), ((), ())), preferred_element_type=jnp.float32)
+    back = lax.psum(back.astype(jnp.bfloat16), "lay").astype(jnp.float32)
+    lat_grad = (back * slope).astype(jnp.bfloat16)
+    enc_grad = lax.dot_general(
+        gathered, lat_grad, (((0,), (0,)), ((), ())), preferred_element_type=jnp.float32
+    ).astype(jnp.bfloat16)
+    return lat_grad, enc_grad, code, err
+
+
+def build(step):
+    def on_device(acts, w_enc, w_dec, b_enc, b_dec):
         row_dev, lay_dev, width = acts.shape
         lat_dev = w_enc.shape[2]
         flat = lay_dev * width
-        own = acts.reshape(row_dev, flat)
-        we = w_enc.reshape(flat, lat_dev)
-        wd = w_dec.reshape(lat_dev, flat)
-        bd = b_dec.reshape(1, flat)
-        near = direct(lat) and direct(lay)
-        if near:
-            blocks = gather_blocks(own, "lat", lat)
-            blocks[0], we = keep_near(own, we)
-            term = product(blocks, we)
-            acts_t = turned(blocks)
-            wd_t = turned([wd])
-        else:
-            gathered = lax.all_gather(own, "lat", axis=0, tiled=True)
-            term = jnp.dot(gathered, we, preferred_element_type=jnp.float32)
-        pre = all_sum(term.astype(jnp.bfloat16), "lay", lay) + b_enc[None, :]
-        code = (jax.nn.softplus(4.0 * pre) / 4.0).astype(jnp.bfloat16)
-        slope = jax.nn.sigmoid(4.0 * pre)
-        part = jnp.dot(code, wd, preferred_element_type=jnp.float32).astype(jnp.bfloat16)
-        if near:
-            pieces = part.reshape(lat, row_dev, flat)
-            mine = pair_sum(
-                [pieces[0].astype(jnp.float32)]
-                + [swap(pieces[k], "lat", lat, k).astype(jnp.float32) for k in range(1, lat)]
-            )
-        else:
-            mine = lax.psum_scatter(part, "lat", scatter_dimension=0, tiled=True).astype(jnp.float32)
-        err_own = (mine + bd - own.astype(jnp.float32)).astype(jnp.bfloat16)
-        if near:
-            errs = gather_blocks(err_own, "lat", lat)
-            back = product(errs, wd_t)
-            err = jnp.concatenate(errs, axis=0)
-        else:
-            err = lax.all_gather(err_own, "lat", axis=0, tiled=True)
-            back = lax.dot_general(
-                err, wd, (((1,), (1,)), ((), ())), preferred_element_type=jnp.float32
-            ).astype(jnp.bfloat16)
-        if near:
-            lat_grad, enc_grad = last_stage(gather_blocks(back, "lay", lay), slope, acts_t, lat)
-        else:
-            lat_grad = (lax.psum(back, "lay").astype(jnp.float32) * slope).astype(jnp.bfloat16)
-            enc_grad = lax.dot_general(
-                gathered, lat_grad, (((0,), (0,)), ((), ())), preferred_element_type=jnp.float32
-            ).astype(jnp.bfloat16)
+        lat_grad, enc_grad, code, err = step(
+            acts.reshape(row_dev, flat),
+            w_enc.reshape(flat, lat_dev),
+            w_dec.reshape(lat_dev, flat),
+            b_enc.reshape(1, lat_dev),
+            b_dec.reshape(1, flat),
+        )
         dec_grad = lax.dot_general(
             code, err, (((0,), (0,)), ((), ())), preferred_element_type=jnp.float32
         ).astype(jnp.bfloat16)
@@ -200,7 +241,7 @@
             dec_grad.reshape(lat_dev, lay_dev, width),
         )
 
-    return step
+    return on_device
 
 
 def solution(mesh):
@@ -213,6 +254,11 @@
     )
     out_specs = (P("grp", "lat"), P(("grp", "lay"), None, "lat"), P("lat", ("grp", "lay"), None))
     lat, lay = mesh.shape["lat"], mesh.shape["lay"]
+    near = direct(lat) and direct(lay)
     return jax.shard_map(
-        build(lat, lay), mesh=mesh, in_specs=in_specs, out_specs=out_specs, check_vma=False
+        build(near_step(lat, lay) if near else far_step),
+        mesh=mesh,
+        in_specs=in_specs,
+        out_specs=out_specs,
+        check_vma=False,
     )

time: 38.3 us -> 38.3 us (level)
  waiting for transfers between devices: 14.5 us -> 13.9 us
  starting transfers between devices: 17.6 us -> 18.2 us
  Pallas kernels: 3.46 us -> 3.89 us
    ppermute x0 -> x8, starting transfers between devices: none -> 8.57 us  [cross(): return lax.ppermute(x, ('lat', 'lay'), pairs)]
    ppermute x15 -> x9, starting transfers between devices: 17.6 us -> 9.63 us  [swap(): return lax.ppermute(x, axis, [(a, a ^ step) for a in range(size)])]
    ppermute x15 -> x9, waiting for transfers between devices: 14.5 us -> 8.04 us  [swap(): return lax.ppermute(x, axis, [(a, a ^ step) for a in range(size)])]
    ppermute x0 -> x8, waiting for transfers between devices: none -> 5.87 us  [cross(): return lax.ppermute(x, ('lat', 'lay'), pairs)]
    dot_general x2 -> x1, matrix products: 1.66 us -> 1.39 us  [on_device(): lax.dot_general(code, err, (((0,), (0,)), ((), ())), preferred_element_ty...]
  transfers between devices with their start and end apart: 15 -> 17, of which waited for: 11 -> 10; matrix products, arithmetic and copies ran while one was open for 4% -> 4% of each run, Pallas kernels for 4% -> 5%
where the time goes in v1:
time: 38.3 us; the launch traced here: 38.1 us
  starting transfers between devices  18.2 us (48%)
  waiting for transfers between devices  13.9 us (36%)
  Pallas kernels  3.89 us (10%)
  matrix products  1.39 us (4%)
  between operations  0.71 us (2%)
    ppermute x9, starting transfers between devices, swap(): return lax.ppermute(x, axis, [(a, a ^ step) for a in range(size)])  9.63 us
    ppermute x8, starting transfers between devices, cross(): return lax.ppermute(x, ('lat', 'lay'), pairs)  8.57 us
    ppermute x9, waiting for transfers between devices, swap(): return lax.ppermute(x, axis, [(a, a ^ step) for a in range(size)])  8.04 us
    ppermute x8, waiting for transfers between devices, cross(): return lax.ppermute(x, ('lat', 'lay'), pairs)  5.87 us
    dot_general x1, matrix products, on_device(): lax.dot_general(code, err, (((0,), (0,)), ((), ())), preferred_element_ty...  1.39 us
    pallas_call x1, Pallas kernels, keep_near(): pl.pallas_call(kernel, out_shape=[jax.ShapeDtypeStruct(a.shape, a.dtype)...  1.33 us
    pallas_call x1, Pallas kernels, last_stage(): pl.pallas_call(kernel, out_shape=(jax.ShapeDtypeStruct((rows, lat_dev), j...  1.2 us
  transfers between devices with their start and end apart: 17, of which 10 were waited for; matrix products, arithmetic and copies ran while one was open for 4% of the time, Pallas kernels for 5%

profile of v1, /device:TPU:0, one launch (start us, length us, event | category | flops | bytes accessed | tf_op | source)
XLA Modules:
  0.0 38.1 jit_solution(16791332106364620031)
XLA Ops:
  0.6 5.1 %collective-permute-start.2 = (bf16[16,1280]{1,0:T(8,128)(2,1)}, bf16[16,1280]{1,0:T(8,128)(2,1)S(1)}, u32[]{:S(2)}, u32[]{:S(2)}) collective-permute-start(bf16[16,1280]{1,0:T(8,128)(2,1)} %bitcast.10), channel_id=1, source_target_pairs={{0,12},{4,8},{8,4},{12,0},{1,13},{5,9},{9,5},{13,1},{2,14},{6,10},... | collective-permute-start | bytes 122888 | tf_op jit(solution)/shard_map/ppermute | solution.py:17
  5.8 0.0 collective-permute-start.1
  5.8 0.6 %collective-permute-start = (bf16[16,1280]{1,0:T(8,128)(2,1)}, bf16[16,1280]{1,0:T(8,128)(2,1)S(1)}, u32[]{:S(2)}, u32[]{:S(2)}) collective-permute-start(bf16[16,1280]{1,0:T(8,128)(2,1)} %bitcast.12), channel_id=1, source_target_pairs={{0,4},{4,0},{8,12},{12,8},{1,5},{5,1},{9,13},{13,9},{2,6},{6,2},{1... | collective-permute-start | bytes 122888 | tf_op jit(solution)/shard_map/ppermute | solution.py:17
  6.4 0.0 copy-start.2
  6.4 0.0 copy-start
  6.4 0.0 copy-start.1
  6.4 1.3 %keep_near.1 = (bf16[16,1280]{1,0:T(8,128)(2,1)S(1)}, bf16[1280,384]{1,0:T(8,128)(2,1)S(1)}) custom-call(bf16[16,1280]{1,0:T(8,128)(2,1)} %bitcast.13, bf16[1280,384]{1,0:T(8,128)(2,1)} %bitcast.9), custom_call_target="tpu_custom_call" | custom-call | tf_op jit(solution)/shard_map/keep_near/pallas_call | solution.py:56
  7.8 0.2 collective-permute-done.2.refs_3_
  8.0 2.9 %collective-permute-done.1.refs_2_ = bf16[16,1280]{1,0:T(8,128)(2,1)S(1)} collective-permute-done((bf16[16,1280]{1,0:T(8,128)(2,1)}, bf16[16,1280]{1,0:T(8,128)(2,1)S(1)}, u32[]{:S(2)}, u32[]{:S(2)}) %collective-permute-start.1) | collective-permute-done | bytes 40992 | tf_op jit(solution)/shard_map/ppermute | solution.py:17
  10.9 0.0 collective-permute-done.refs_1_
  10.9 0.3 product.2.refs_0_
  11.2 0.1 collective-permute-start.5
  11.3 1.6 %collective-permute-start.4 = (bf16[64,384]{1,0:T(8,128)(2,1)S(1)}, bf16[64,384]{1,0:T(8,128)(2,1)S(1)}, u32[]{:S(2)}, u32[]{:S(2)}) collective-permute-start(bf16[64,384]{1,0:T(8,128)(2,1)S(1)} %product.2.refs_0_), channel_id=1, source_target_pairs={{0,2},{1,3},{2,0},{3,1},{4,6},{5,7},{6,4},{7,5},{8,10},{9,11},{10,... | collective-permute-start | bytes 147464 | tf_op jit(solution)/shard_map/ppermute | solution.py:17
  12.8 0.3 collective-permute-start.3
  13.1 0.0 copy-done.2
  13.1 2.1 %collective-permute-done.5.refs_3_ = bf16[64,384]{1,0:T(8,128)(2,1)S(1)} collective-permute-done((bf16[64,384]{1,0:T(8,128)(2,1)S(1)}, bf16[64,384]{1,0:T(8,128)(2,1)S(1)}, u32[]{:S(2)}, u32[]{:S(2)}) %collective-permute-start.5) | collective-permute-done | bytes 49184 | tf_op jit(solution)/shard_map/ppermute | solution.py:17
  15.2 0.9 %collective-permute-done.4.refs_2_ = bf16[64,384]{1,0:T(8,128)(2,1)S(1)} collective-permute-done((bf16[64,384]{1,0:T(8,128)(2,1)S(1)}, bf16[64,384]{1,0:T(8,128)(2,1)S(1)}, u32[]{:S(2)}, u32[]{:S(2)}) %collective-permute-start.4) | collective-permute-done | bytes 49184 | tf_op jit(solution)/shard_map/ppermute | solution.py:17
  16.2 0.0 collective-permute-done.3.refs_1_
  16.2 0.0 copy-done
  16.2 0.0 copy-done.1
  16.2 0.3 recon_pieces.1
  16.5 0.2 collective-permute-start.6
  16.7 0.2 collective-permute-start.7
  16.9 1.9 %collective-permute-start.8 = (bf16[16,1280]{1,0:T(8,128)(2,1)S(1)}, bf16[16,1280]{1,0:T(8,128)(2,1)S(1)}, u32[]{:S(2)}, u32[]{:S(2)}) collective-permute-start(bf16[16,1280]{1,0:T(8,128)(2,1)S(1)} %get-tuple-element.17), channel_id=1, source_target_pairs={{0,9},{1,8},{2,11},{3,10},{4,13},{5,12},{6,15},{7,14},{8,1},{9,0},... | collective-permute-start | bytes 122888 | tf_op jit(solution)/shard_map/ppermute | solution.py:28
  18.7 2.1 %collective-permute-start.9 = (bf16[16,1280]{1,0:T(8,128)(2,1)S(1)}, bf16[16,1280]{1,0:T(8,128)(2,1)S(1)}, u32[]{:S(2)}, u32[]{:S(2)}) collective-permute-start(bf16[16,1280]{1,0:T(8,128)(2,1)S(1)} %get-tuple-element.18), channel_id=1, source_target_pairs={{0,13},{1,12},{2,15},{3,14},{4,9},{5,8},{6,11},{7,10},{8,5},{9,4},... | collective-permute-start | bytes 122888 | tf_op jit(solution)/shard_map/ppermute | solution.py:28
  20.8 0.0 collective-permute-done.6
  20.8 0.0 collective-permute-done.7
  20.8 0.4 collective-permute-done.8
  21.2 2.9 %collective-permute-done.9 = bf16[16,1280]{1,0:T(8,128)(2,1)S(1)} collective-permute-done((bf16[16,1280]{1,0:T(8,128)(2,1)S(1)}, bf16[16,1280]{1,0:T(8,128)(2,1)S(1)}, u32[]{:S(2)}, u32[]{:S(2)}) %collective-permute-start.9) | collective-permute-done | bytes 40992 | tf_op jit(solution)/shard_map/ppermute | solution.py:28
  24.1 2.0 %collective-permute-start.13 = (bf16[16,1280]{1,0:T(8,128)(2,1)S(1)}, bf16[16,1280]{1,0:T(8,128)(2,1)S(1)}, u32[]{:S(2)}, u32[]{:S(2)}) collective-permute-start(bf16[16,1280]{1,0:T(8,128)(2,1)S(1)} %add_convert_fusion), channel_id=1, source_target_pairs={{0,13},{1,12},{2,15},{3,14},{4,9},{5,8},{6,11},{7,10},{8,5},{9,4},... | collective-permute-start | bytes 122888 | tf_op jit(solution)/shard_map/ppermute | solution.py:28
  26.1 0.0 collective-permute-start.12
  26.2 2.0 %collective-permute-start.11 = (bf16[16,1280]{1,0:T(8,128)(2,1)S(1)}, bf16[16,1280]{1,0:T(8,128)(2,1)S(1)}, u32[]{:S(2)}, u32[]{:S(2)}) collective-permute-start(bf16[16,1280]{1,0:T(8,128)(2,1)S(1)} %add_convert_fusion), channel_id=1, source_target_pairs={{0,5},{1,4},{2,7},{3,6},{4,1},{5,0},{6,3},{7,2},{8,13},{9,12},{10,... | collective-permute-start | bytes 122888 | tf_op jit(solution)/shard_map/ppermute | solution.py:28
  28.1 0.3 collective-permute-start.10
  28.4 0.3 turned.2.refs_4_
  28.7 0.1 turned.3.refs_5_
  28.9 0.6 %collective-permute-done.13.refs_3_ = bf16[16,1280]{1,0:T(8,128)(2,1)S(1)} collective-permute-done((bf16[16,1280]{1,0:T(8,128)(2,1)S(1)}, bf16[16,1280]{1,0:T(8,128)(2,1)S(1)}, u32[]{:S(2)}, u32[]{:S(2)}) %collective-permute-start.13) | collective-permute-done | bytes 40992 | tf_op jit(solution)/shard_map/ppermute | solution.py:28
  29.4 2.0 %collective-permute-done.12.refs_2_ = bf16[16,1280]{1,0:T(8,128)(2,1)S(1)} collective-permute-done((bf16[16,1280]{1,0:T(8,128)(2,1)S(1)}, bf16[16,1280]{1,0:T(8,128)(2,1)S(1)}, u32[]{:S(2)}, u32[]{:S(2)}) %collective-permute-start.12) | collective-permute-done | bytes 40992 | tf_op jit(solution)/shard_map/ppermute | solution.py:28
  31.5 0.0 collective-permute-done.11.refs_1_
  31.5 0.0 collective-permute-done.10.refs_0_
  31.5 0.3 product.3.refs_0_
  31.8 0.9 %collective-permute-start.16 = (bf16[64,384]{1,0:T(8,128)(2,1)S(1)}, bf16[64,384]{1,0:T(8,128)(2,1)S(1)}, u32[]{:S(2)}, u32[]{:S(2)}) collective-permute-start(bf16[64,384]{1,0:T(8,128)(2,1)S(1)} %product.3.refs_0_), channel_id=1, source_target_pairs={{0,3},{1,2},{2,1},{3,0},{4,7},{5,6},{6,5},{7,4},{8,11},{9,10},{10,... | collective-permute-start | bytes 147464 | tf_op jit(solution)/shard_map/ppermute | solution.py:17
  32.7 0.9 %collective-permute-start.15 = (bf16[64,384]{1,0:T(8,128)(2,1)S(1)}, bf16[64,384]{1,0:T(8,128)(2,1)S(1)}, u32[]{:S(2)}, u32[]{:S(2)}) collective-permute-start(bf16[64,384]{1,0:T(8,128)(2,1)S(1)} %product.3.refs_0_), channel_id=1, source_target_pairs={{0,2},{1,3},{2,0},{3,1},{4,6},{5,7},{6,4},{7,5},{8,10},{9,11},{10,... | collective-permute-start | bytes 147464 | tf_op jit(solution)/shard_map/ppermute | solution.py:17
  33.6 0.1 collective-permute-start.14
  33.7 1.4 %fusion = bf16[384,1,1280]{2,0,1:T(8,128)(2,1)} fusion(bf16[64,384]{1,0:T(8,128)(2,1)S(1)} %get-tuple-element.22, bf16[16,1280]{1,0:T(8,128)(2,1)S(1)} %collective-permute-done.13.refs_3_, bf16[16,1280]{1,0:T(8,128)(2,1)S(1)} %collective-permute-done.12.refs_2_, bf16[16,1280]{1,0:T(8,128)(2,1)S(1)} %collective-permute-done.11.refs_1_, ...), kind=kOutput, calls=%fused_computation.1 | convolution fusion | flops 64061440 | bytes 1196032 | tf_op jit(solution)/shard_map/dot_general | solution.py:235
  35.1 0.5 %collective-permute-done.16.refs_3_ = bf16[64,384]{1,0:T(8,128)(2,1)S(1)} collective-permute-done((bf16[64,384]{1,0:T(8,128)(2,1)S(1)}, bf16[64,384]{1,0:T(8,128)(2,1)S(1)}, u32[]{:S(2)}, u32[]{:S(2)}) %collective-permute-start.16) | collective-permute-done | bytes 49184 | tf_op jit(solution)/shard_map/ppermute | solution.py:17
  35.6 1.3 %collective-permute-done.15.refs_2_ = bf16[64,384]{1,0:T(8,128)(2,1)S(1)} collective-permute-done((bf16[64,384]{1,0:T(8,128)(2,1)S(1)}, bf16[64,384]{1,0:T(8,128)(2,1)S(1)}, u32[]{:S(2)}, u32[]{:S(2)}) %collective-permute-start.15) | collective-permute-done | bytes 49184 | tf_op jit(solution)/shard_map/ppermute | solution.py:17
  36.9 0.0 collective-permute-done.14.refs_1_
  36.9 1.2 %last_stage.1 = (bf16[64,384]{1,0:T(8,128)(2,1)}, bf16[1280,384]{1,0:T(8,128)(2,1)}) custom-call(bf16[64,384]{1,0:T(8,128)(2,1)S(1)} %product.3.refs_0_, bf16[64,384]{1,0:T(8,128)(2,1)S(1)} %collective-permute-done.14.refs_1_, bf16[64,384]{1,0:T(8,128)(2,1)S(1)} %collective-permute-done.15.refs_2_, bf16[64,384]{1,0:T(8,128)(2,1)S(1)} %collective-permute-done.16.refs_3_, ...), custom_call_target="tpu_custom_call" | custom-call | tf_op jit(solution)/shard_map/last_stage/pallas_call | solution.py:167
  (2 shorter events, 0.0 us)
Async XLA Ops:
  0.6 7.3 %collective-permute-start.2 = (bf16[16,1280]{1,0:T(8,128)(2,1)}, bf16[16,1280]{1,0:T(8,128)(2,1)S(1)}, u32[]{:S(2)}, u32[]{:S(2)}) collective-permute-start(bf16[16,1280]{1,0:T(8,128)(2,1)} %bitcast.10), channel_id=1, source_target_pairs={{0,12},{4,8},{8,4},{12,0},{1,13},{5,9},{9,5},{13,1},{2,14},{6,10},... | collective-permute-start | bytes 122888 | tf_op jit(solution)/shard_map/ppermute | solution.py:17
  5.8 5.1 %collective-permute-start.1 = (bf16[16,1280]{1,0:T(8,128)(2,1)}, bf16[16,1280]{1,0:T(8,128)(2,1)S(1)}, u32[]{:S(2)}, u32[]{:S(2)}) collective-permute-start(bf16[16,1280]{1,0:T(8,128)(2,1)} %bitcast.11), channel_id=1, source_target_pairs={{0,8},{4,12},{8,0},{12,4},{1,9},{5,13},{9,1},{13,5},{2,10},{6,14},... | collective-permute-start | bytes 122888 | tf_op jit(solution)/shard_map/ppermute | solution.py:17
  5.8 5.1 %collective-permute-start = (bf16[16,1280]{1,0:T(8,128)(2,1)}, bf16[16,1280]{1,0:T(8,128)(2,1)S(1)}, u32[]{:S(2)}, u32[]{:S(2)}) collective-permute-start(bf16[16,1280]{1,0:T(8,128)(2,1)} %bitcast.12), channel_id=1, source_target_pairs={{0,4},{4,0},{8,12},{12,8},{1,5},{5,1},{9,13},{13,9},{2,6},{6,2},{1... | collective-permute-start | bytes 122888 | tf_op jit(solution)/shard_map/ppermute | solution.py:17
  6.4 6.7 %copy-start.2 = (f32[384]{0:T(512)S(1)}, f32[384]{0:T(512)}, u32[]{:S(2)}) copy-start(f32[384]{0:T(512)} %param.8) | copy-start | bytes 4612
  6.4 9.8 %copy-start = (bf16[384,1,1280]{2,0,1:T(8,128)(2,1)S(1)}, bf16[384,1,1280]{2,0,1:T(8,128)(2,1)}, u32[]{:S(2)}) copy-start(bf16[384,1,1280]{2,0,1:T(8,128)(2,1)} %param.7) | copy-start | bytes 2949124
  6.4 9.8 %copy-start.1 = (f32[1,1280]{1,0:T(1,128)S(1)}, f32[1,1280]{1,0:T(1,128)}, u32[]{:S(2)}) copy-start(f32[1,1280]{1,0:T(1,128)} %refs_7_.1) | copy-start | bytes 15364
  11.2 4.1 %collective-permute-start.5 = (bf16[64,384]{1,0:T(8,128)(2,1)S(1)}, bf16[64,384]{1,0:T(8,128)(2,1)S(1)}, u32[]{:S(2)}, u32[]{:S(2)}) collective-permute-start(bf16[64,384]{1,0:T(8,128)(2,1)S(1)} %product.2.refs_0_), channel_id=1, source_target_pairs={{0,3},{1,2},{2,1},{3,0},{4,7},{5,6},{6,5},{7,4},{8,11},{9,10},{10,... | collective-permute-start | bytes 147464 | tf_op jit(solution)/shard_map/ppermute | solution.py:17
  11.3 4.9 %collective-permute-start.4 = (bf16[64,384]{1,0:T(8,128)(2,1)S(1)}, bf16[64,384]{1,0:T(8,128)(2,1)S(1)}, u32[]{:S(2)}, u32[]{:S(2)}) collective-permute-start(bf16[64,384]{1,0:T(8,128)(2,1)S(1)} %product.2.refs_0_), channel_id=1, source_target_pairs={{0,2},{1,3},{2,0},{3,1},{4,6},{5,7},{6,4},{7,5},{8,10},{9,11},{10,... | collective-permute-start | bytes 147464 | tf_op jit(solution)/shard_map/ppermute | solution.py:17
  12.8 3.4 %collective-permute-start.3 = (bf16[64,384]{1,0:T(8,128)(2,1)S(1)}, bf16[64,384]{1,0:T(8,128)(2,1)S(1)}, u32[]{:S(2)}, u32[]{:S(2)}) collective-permute-start(bf16[64,384]{1,0:T(8,128)(2,1)S(1)} %product.2.refs_0_), channel_id=1, source_target_pairs={{0,1},{1,0},{2,3},{3,2},{4,5},{5,4},{6,7},{7,6},{8,9},{9,8},{10,11... | collective-permute-start | bytes 147464 | tf_op jit(solution)/shard_map/ppermute | solution.py:17
  16.5 4.3 %collective-permute-start.6 = (bf16[16,1280]{1,0:T(8,128)(2,1)S(1)}, bf16[16,1280]{1,0:T(8,128)(2,1)S(1)}, u32[]{:S(2)}, u32[]{:S(2)}) collective-permute-start(bf16[16,1280]{1,0:T(8,128)(2,1)S(1)} %get-tuple-element.15), channel_id=1, source_target_pairs={{0,1},{1,0},{2,3},{3,2},{4,5},{5,4},{6,7},{7,6},{8,9},{9,8},{10,11... | collective-permute-start | bytes 122888 | tf_op jit(solution)/shard_map/ppermute | solution.py:28
  16.7 4.1 %collective-permute-start.7 = (bf16[16,1280]{1,0:T(8,128)(2,1)S(1)}, bf16[16,1280]{1,0:T(8,128)(2,1)S(1)}, u32[]{:S(2)}, u32[]{:S(2)}) collective-permute-start(bf16[16,1280]{1,0:T(8,128)(2,1)S(1)} %get-tuple-element.16), channel_id=1, source_target_pairs={{0,5},{1,4},{2,7},{3,6},{4,1},{5,0},{6,3},{7,2},{8,13},{9,12},{10,... | collective-permute-start | bytes 122888 | tf_op jit(solution)/shard_map/ppermute | solution.py:28
  16.9 4.3 %collective-permute-start.8 = (bf16[16,1280]{1,0:T(8,128)(2,1)S(1)}, bf16[16,1280]{1,0:T(8,128)(2,1)S(1)}, u32[]{:S(2)}, u32[]{:S(2)}) collective-permute-start(bf16[16,1280]{1,0:T(8,128)(2,1)S(1)} %get-tuple-element.17), channel_id=1, source_target_pairs={{0,9},{1,8},{2,11},{3,10},{4,13},{5,12},{6,15},{7,14},{8,1},{9,0},... | collective-permute-start | bytes 122888 | tf_op jit(solution)/shard_map/ppermute | solution.py:28
  18.7 5.4 %collective-permute-start.9 = (bf16[16,1280]{1,0:T(8,128)(2,1)S(1)}, bf16[16,1280]{1,0:T(8,128)(2,1)S(1)}, u32[]{:S(2)}, u32[]{:S(2)}) collective-permute-start(bf16[16,1280]{1,0:T(8,128)(2,1)S(1)} %get-tuple-element.18), channel_id=1, source_target_pairs={{0,13},{1,12},{2,15},{3,14},{4,9},{5,8},{6,11},{7,10},{8,5},{9,4},... | collective-permute-start | bytes 122888 | tf_op jit(solution)/shard_map/ppermute | solution.py:28
  24.1 5.3 %collective-permute-start.13 = (bf16[16,1280]{1,0:T(8,128)(2,1)S(1)}, bf16[16,1280]{1,0:T(8,128)(2,1)S(1)}, u32[]{:S(2)}, u32[]{:S(2)}) collective-permute-start(bf16[16,1280]{1,0:T(8,128)(2,1)S(1)} %add_convert_fusion), channel_id=1, source_target_pairs={{0,13},{1,12},{2,15},{3,14},{4,9},{5,8},{6,11},{7,10},{8,5},{9,4},... | collective-permute-start | bytes 122888 | tf_op jit(solution)/shard_map/ppermute | solution.py:28
  26.1 5.3 %collective-permute-start.12 = (bf16[16,1280]{1,0:T(8,128)(2,1)S(1)}, bf16[16,1280]{1,0:T(8,128)(2,1)S(1)}, u32[]{:S(2)}, u32[]{:S(2)}) collective-permute-start(bf16[16,1280]{1,0:T(8,128)(2,1)S(1)} %add_convert_fusion), channel_id=1, source_target_pairs={{0,9},{1,8},{2,11},{3,10},{4,13},{5,12},{6,15},{7,14},{8,1},{9,0},... | collective-permute-start | bytes 122888 | tf_op jit(solution)/shard_map/ppermute | solution.py:28
  26.2 5.3 %collective-permute-start.11 = (bf16[16,1280]{1,0:T(8,128)(2,1)S(1)}, bf16[16,1280]{1,0:T(8,128)(2,1)S(1)}, u32[]{:S(2)}, u32[]{:S(2)}) collective-permute-start(bf16[16,1280]{1,0:T(8,128)(2,1)S(1)} %add_convert_fusion), channel_id=1, source_target_pairs={{0,5},{1,4},{2,7},{3,6},{4,1},{5,0},{6,3},{7,2},{8,13},{9,12},{10,... | collective-permute-start | bytes 122888 | tf_op jit(solution)/shard_map/ppermute | solution.py:28
  28.1 3.3 %collective-permute-start.10 = (bf16[16,1280]{1,0:T(8,128)(2,1)S(1)}, bf16[16,1280]{1,0:T(8,128)(2,1)S(1)}, u32[]{:S(2)}, u32[]{:S(2)}) collective-permute-start(bf16[16,1280]{1,0:T(8,128)(2,1)S(1)} %add_convert_fusion), channel_id=1, source_target_pairs={{0,1},{1,0},{2,3},{3,2},{4,5},{5,4},{6,7},{7,6},{8,9},{9,8},{10,11... | collective-permute-start | bytes 122888 | tf_op jit(solution)/shard_map/ppermute | solution.py:28
  31.8 3.8 %collective-permute-start.16 = (bf16[64,384]{1,0:T(8,128)(2,1)S(1)}, bf16[64,384]{1,0:T(8,128)(2,1)S(1)}, u32[]{:S(2)}, u32[]{:S(2)}) collective-permute-start(bf16[64,384]{1,0:T(8,128)(2,1)S(1)} %product.3.refs_0_), channel_id=1, source_target_pairs={{0,3},{1,2},{2,1},{3,0},{4,7},{5,6},{6,5},{7,4},{8,11},{9,10},{10,... | collective-permute-start | bytes 147464 | tf_op jit(solution)/shard_map/ppermute | solution.py:17
  32.7 4.2 %collective-permute-start.15 = (bf16[64,384]{1,0:T(8,128)(2,1)S(1)}, bf16[64,384]{1,0:T(8,128)(2,1)S(1)}, u32[]{:S(2)}, u32[]{:S(2)}) collective-permute-start(bf16[64,384]{1,0:T(8,128)(2,1)S(1)} %product.3.refs_0_), channel_id=1, source_target_pairs={{0,2},{1,3},{2,0},{3,1},{4,6},{5,7},{6,4},{7,5},{8,10},{9,11},{10,... | collective-permute-start | bytes 147464 | tf_op jit(solution)/shard_map/ppermute | solution.py:17
  33.6 3.4 %collective-permute-start.14 = (bf16[64,384]{1,0:T(8,128)(2,1)S(1)}, bf16[64,384]{1,0:T(8,128)(2,1)S(1)}, u32[]{:S(2)}, u32[]{:S(2)}) collective-permute-start(bf16[64,384]{1,0:T(8,128)(2,1)S(1)} %product.3.refs_0_), channel_id=1, source_target_pairs={{0,1},{1,0},{2,3},{3,2},{4,5},{5,4},{6,7},{7,6},{8,9},{9,8},{10,11... | collective-permute-start | bytes 147464 | tf_op jit(solution)/shard_map/ppermute | solution.py:17

commit v2 on v1

--- a/solution.py
+++ b/solution.py
@@ -108,10 +108,11 @@
         )
         pre = pair_sum([r[...].astype(jnp.float32) for r in t_refs]) + b_enc_ref[...]
         x = 4.0 * pre
-        soft = jnp.maximum(x, 0.0) + jnp.log1p(jnp.exp(-jnp.abs(x)))
+        small = jnp.exp(-jnp.abs(x))
+        soft = jnp.maximum(x, 0.0) + jnp.log1p(small)
         code = (soft * 0.25).astype(jnp.bfloat16)
         code_ref[...] = code
-        slope_ref[...] = jax.nn.sigmoid(x)
+        slope_ref[...] = jnp.where(x >= 0.0, 1.0, small) / (1.0 + small)
         part = jnp.dot(code, wd_ref[...], preferred_element_type=jnp.float32)
         for k, ref in enumerate(piece_refs):
             piece = part[k * row_dev : (k + 1) * row_dev]
@@ -138,7 +139,8 @@
 def last_stage(backs, slope, acts_t, lat):
     rows, lat_dev = slope.shape
     row_dev, depth = rows // lat, acts_t.shape[0]
-    step = depth // BLOCKS
+    parts = BLOCKS if depth % (16 * BLOCKS) == 0 else 1
+    step = depth // parts
     count = len(backs)
 
     def kernel(*refs):
@@ -152,9 +154,9 @@
         for k in range(lat):
             at = pl.multiple_of(lax.bitwise_xor(me, k) * row_dev, row_dev)
             grad_held[pl.ds(at, row_dev), :] = grad[k * row_dev : (k + 1) * row_dev]
-        copies = [pltpu.make_async_copy(grad_held, grad_ref, sems.at[BLOCKS])]
+        copies = [pltpu.make_async_copy(grad_held, grad_ref, sems.at[parts])]
         copies[0].start()
-        for n in range(BLOCKS):
+        for n in range(parts):
             part = pl.ds(n * step, step)
             held[part, :] = jnp.dot(
                 x_ref[part, :], grad, preferred_element_type=jnp.float32
@@ -175,7 +177,7 @@
         scratch_shapes=[
             pltpu.VMEM((rows, lat_dev), jnp.bfloat16),
             pltpu.VMEM((depth, lat_dev), jnp.bfloat16),
-            pltpu.SemaphoreType.DMA((BLOCKS + 1,)),
+            pltpu.SemaphoreType.DMA((parts + 1,)),
         ],
         compiler_params=SMALL,
         name="last_stage",

time: 38.3 us -> 38.3 us (level)
  no operation moved by 1% of the time
where the time goes in v2:
time: 38.3 us; the launch traced here: 38.1 us
  starting transfers between devices  18.2 us (48%)
  waiting for transfers between devices  13.9 us (36%)
  Pallas kernels  3.89 us (10%)
  matrix products  1.39 us (4%)
  between operations  0.7 us (2%)
    ppermute x9, starting transfers between devices, swap(): return lax.ppermute(x, axis, [(a, a ^ step) for a in range(size)])  9.63 us
    ppermute x8, starting transfers between devices, cross(): return lax.ppermute(x, ('lat', 'lay'), pairs)  8.57 us
    ppermute x9, waiting for transfers between devices, swap(): return lax.ppermute(x, axis, [(a, a ^ step) for a in range(size)])  8.05 us
    ppermute x8, waiting for transfers between devices, cross(): return lax.ppermute(x, ('lat', 'lay'), pairs)  5.86 us
    dot_general x1, matrix products, on_device(): lax.dot_general(code, err, (((0,), (0,)), ((), ())), preferred_element_ty...  1.39 us
    pallas_call x1, Pallas kernels, keep_near(): pl.pallas_call(kernel, out_shape=[jax.ShapeDtypeStruct(a.shape, a.dtype)...  1.33 us
    pallas_call x1, Pallas kernels, last_stage(): pl.pallas_call(kernel, out_shape=(jax.ShapeDtypeStruct((rows, lat_dev), j...  1.19 us
  transfers between devices with their start and end apart: 17, of which 10 were waited for; matrix products, arithmetic and copies ran while one was open for 4% of the time, Pallas kernels for 5%

profile of v2, /device:TPU:0, one launch (start us, length us, event | category | flops | bytes accessed | tf_op | source)
XLA Modules:
  0.0 38.1 jit_solution(7797684028414013231)
XLA Ops:
  0.6 5.1 %collective-permute-start.2 = (bf16[16,1280]{1,0:T(8,128)(2,1)}, bf16[16,1280]{1,0:T(8,128)(2,1)S(1)}, u32[]{:S(2)}, u32[]{:S(2)}) collective-permute-start(bf16[16,1280]{1,0:T(8,128)(2,1)} %bitcast.10), channel_id=1, source_target_pairs={{0,12},{4,8},{8,4},{12,0},{1,13},{5,9},{9,5},{13,1},{2,14},{6,10},... | collective-permute-start | bytes 122888 | tf_op jit(solution)/shard_map/ppermute | solution.py:17
  5.8 0.0 collective-permute-start.1
  5.8 0.6 %collective-permute-start = (bf16[16,1280]{1,0:T(8,128)(2,1)}, bf16[16,1280]{1,0:T(8,128)(2,1)S(1)}, u32[]{:S(2)}, u32[]{:S(2)}) collective-permute-start(bf16[16,1280]{1,0:T(8,128)(2,1)} %bitcast.12), channel_id=1, source_target_pairs={{0,4},{4,0},{8,12},{12,8},{1,5},{5,1},{9,13},{13,9},{2,6},{6,2},{1... | collective-permute-start | bytes 122888 | tf_op jit(solution)/shard_map/ppermute | solution.py:17
  6.4 0.0 copy-start.2
  6.4 0.0 copy-start
  6.4 0.0 copy-start.1
  6.4 1.3 %keep_near.1 = (bf16[16,1280]{1,0:T(8,128)(2,1)S(1)}, bf16[1280,384]{1,0:T(8,128)(2,1)S(1)}) custom-call(bf16[16,1280]{1,0:T(8,128)(2,1)} %bitcast.13, bf16[1280,384]{1,0:T(8,128)(2,1)} %bitcast.9), custom_call_target="tpu_custom_call" | custom-call | tf_op jit(solution)/shard_map/keep_near/pallas_call | solution.py:56
  7.8 0.2 collective-permute-done.2.refs_3_
  8.0 2.9 %collective-permute-done.1.refs_2_ = bf16[16,1280]{1,0:T(8,128)(2,1)S(1)} collective-permute-done((bf16[16,1280]{1,0:T(8,128)(2,1)}, bf16[16,1280]{1,0:T(8,128)(2,1)S(1)}, u32[]{:S(2)}, u32[]{:S(2)}) %collective-permute-start.1) | collective-permute-done | bytes 40992 | tf_op jit(solution)/shard_map/ppermute | solution.py:17
  10.9 0.0 collective-permute-done.refs_1_
  10.9 0.3 product.2.refs_0_
  11.2 0.1 collective-permute-start.5
  11.3 1.6 %collective-permute-start.4 = (bf16[64,384]{1,0:T(8,128)(2,1)S(1)}, bf16[64,384]{1,0:T(8,128)(2,1)S(1)}, u32[]{:S(2)}, u32[]{:S(2)}) collective-permute-start(bf16[64,384]{1,0:T(8,128)(2,1)S(1)} %product.2.refs_0_), channel_id=1, source_target_pairs={{0,2},{1,3},{2,0},{3,1},{4,6},{5,7},{6,4},{7,5},{8,10},{9,11},{10,... | collective-permute-start | bytes 147464 | tf_op jit(solution)/shard_map/ppermute | solution.py:17
  12.8 0.3 collective-permute-start.3
  13.1 0.0 copy-done.2
  13.1 2.1 %collective-permute-done.5.refs_3_ = bf16[64,384]{1,0:T(8,128)(2,1)S(1)} collective-permute-done((bf16[64,384]{1,0:T(8,128)(2,1)S(1)}, bf16[64,384]{1,0:T(8,128)(2,1)S(1)}, u32[]{:S(2)}, u32[]{:S(2)}) %collective-permute-start.5) | collective-permute-done | bytes 49184 | tf_op jit(solution)/shard_map/ppermute | solution.py:17
  15.2 0.9 %collective-permute-done.4.refs_2_ = bf16[64,384]{1,0:T(8,128)(2,1)S(1)} collective-permute-done((bf16[64,384]{1,0:T(8,128)(2,1)S(1)}, bf16[64,384]{1,0:T(8,128)(2,1)S(1)}, u32[]{:S(2)}, u32[]{:S(2)}) %collective-permute-start.4) | collective-permute-done | bytes 49184 | tf_op jit(solution)/shard_map/ppermute | solution.py:17
  16.2 0.0 collective-permute-done.3.refs_1_
  16.2 0.0 copy-done
  16.2 0.0 copy-done.1
  16.2 0.3 recon_pieces.1
  16.5 0.2 collective-permute-start.6
  16.7 0.2 collective-permute-start.7
  16.9 1.9 %collective-permute-start.8 = (bf16[16,1280]{1,0:T(8,128)(2,1)S(1)}, bf16[16,1280]{1,0:T(8,128)(2,1)S(1)}, u32[]{:S(2)}, u32[]{:S(2)}) collective-permute-start(bf16[16,1280]{1,0:T(8,128)(2,1)S(1)} %get-tuple-element.17), channel_id=1, source_target_pairs={{0,9},{1,8},{2,11},{3,10},{4,13},{5,12},{6,15},{7,14},{8,1},{9,0},... | collective-permute-start | bytes 122888 | tf_op jit(solution)/shard_map/ppermute | solution.py:28
  18.8 2.1 %collective-permute-start.9 = (bf16[16,1280]{1,0:T(8,128)(2,1)S(1)}, bf16[16,1280]{1,0:T(8,128)(2,1)S(1)}, u32[]{:S(2)}, u32[]{:S(2)}) collective-permute-start(bf16[16,1280]{1,0:T(8,128)(2,1)S(1)} %get-tuple-element.18), channel_id=1, source_target_pairs={{0,13},{1,12},{2,15},{3,14},{4,9},{5,8},{6,11},{7,10},{8,5},{9,4},... | collective-permute-start | bytes 122888 | tf_op jit(solution)/shard_map/ppermute | solution.py:28
  20.8 0.0 collective-permute-done.6
  20.8 0.0 collective-permute-done.7
  20.8 0.4 collective-permute-done.8
  21.2 2.9 %collective-permute-done.9 = bf16[16,1280]{1,0:T(8,128)(2,1)S(1)} collective-permute-done((bf16[16,1280]{1,0:T(8,128)(2,1)S(1)}, bf16[16,1280]{1,0:T(8,128)(2,1)S(1)}, u32[]{:S(2)}, u32[]{:S(2)}) %collective-permute-start.9) | collective-permute-done | bytes 40992 | tf_op jit(solution)/shard_map/ppermute | solution.py:28
  24.1 2.0 %collective-permute-start.13 = (bf16[16,1280]{1,0:T(8,128)(2,1)S(1)}, bf16[16,1280]{1,0:T(8,128)(2,1)S(1)}, u32[]{:S(2)}, u32[]{:S(2)}) collective-permute-start(bf16[16,1280]{1,0:T(8,128)(2,1)S(1)} %add_convert_fusion), channel_id=1, source_target_pairs={{0,13},{1,12},{2,15},{3,14},{4,9},{5,8},{6,11},{7,10},{8,5},{9,4},... | collective-permute-start | bytes 122888 | tf_op jit(solution)/shard_map/ppermute | solution.py:28
  26.2 0.0 collective-permute-start.12
  26.2 2.0 %collective-permute-start.11 = (bf16[16,1280]{1,0:T(8,128)(2,1)S(1)}, bf16[16,1280]{1,0:T(8,128)(2,1)S(1)}, u32[]{:S(2)}, u32[]{:S(2)}) collective-permute-start(bf16[16,1280]{1,0:T(8,128)(2,1)S(1)} %add_convert_fusion), channel_id=1, source_target_pairs={{0,5},{1,4},{2,7},{3,6},{4,1},{5,0},{6,3},{7,2},{8,13},{9,12},{10,... | collective-permute-start | bytes 122888 | tf_op jit(solution)/shard_map/ppermute | solution.py:28
  28.1 0.3 collective-permute-start.10
  28.4 0.3 turned.2.refs_4_
  28.7 0.1 turned.3.refs_5_
  28.9 0.6 %collective-permute-done.13.refs_3_ = bf16[16,1280]{1,0:T(8,128)(2,1)S(1)} collective-permute-done((bf16[16,1280]{1,0:T(8,128)(2,1)S(1)}, bf16[16,1280]{1,0:T(8,128)(2,1)S(1)}, u32[]{:S(2)}, u32[]{:S(2)}) %collective-permute-start.13) | collective-permute-done | bytes 40992 | tf_op jit(solution)/shard_map/ppermute | solution.py:28
  29.4 2.0 %collective-permute-done.12.refs_2_ = bf16[16,1280]{1,0:T(8,128)(2,1)S(1)} collective-permute-done((bf16[16,1280]{1,0:T(8,128)(2,1)S(1)}, bf16[16,1280]{1,0:T(8,128)(2,1)S(1)}, u32[]{:S(2)}, u32[]{:S(2)}) %collective-permute-start.12) | collective-permute-done | bytes 40992 | tf_op jit(solution)/shard_map/ppermute | solution.py:28
  31.5 0.0 collective-permute-done.11.refs_1_
  31.5 0.0 collective-permute-done.10.refs_0_
  31.5 0.3 product.3.refs_0_
  31.8 1.0 %collective-permute-start.16 = (bf16[64,384]{1,0:T(8,128)(2,1)S(1)}, bf16[64,384]{1,0:T(8,128)(2,1)S(1)}, u32[]{:S(2)}, u32[]{:S(2)}) collective-permute-start(bf16[64,384]{1,0:T(8,128)(2,1)S(1)} %product.3.refs_0_), channel_id=1, source_target_pairs={{0,3},{1,2},{2,1},{3,0},{4,7},{5,6},{6,5},{7,4},{8,11},{9,10},{10,... | collective-permute-start | bytes 147464 | tf_op jit(solution)/shard_map/ppermute | solution.py:17
  32.7 0.9 %collective-permute-start.15 = (bf16[64,384]{1,0:T(8,128)(2,1)S(1)}, bf16[64,384]{1,0:T(8,128)(2,1)S(1)}, u32[]{:S(2)}, u32[]{:S(2)}) collective-permute-start(bf16[64,384]{1,0:T(8,128)(2,1)S(1)} %product.3.refs_0_), channel_id=1, source_target_pairs={{0,2},{1,3},{2,0},{3,1},{4,6},{5,7},{6,4},{7,5},{8,10},{9,11},{10,... | collective-permute-start | bytes 147464 | tf_op jit(solution)/shard_map/ppermute | solution.py:17
  33.6 0.1 collective-permute-start.14
  33.7 1.4 %fusion = bf16[384,1,1280]{2,0,1:T(8,128)(2,1)} fusion(bf16[64,384]{1,0:T(8,128)(2,1)S(1)} %get-tuple-element.22, bf16[16,1280]{1,0:T(8,128)(2,1)S(1)} %collective-permute-done.13.refs_3_, bf16[16,1280]{1,0:T(8,128)(2,1)S(1)} %collective-permute-done.12.refs_2_, bf16[16,1280]{1,0:T(8,128)(2,1)S(1)} %collective-permute-done.11.refs_1_, ...), kind=kOutput, calls=%fused_computation.1 | convolution fusion | flops 64061440 | bytes 1196032 | tf_op jit(solution)/shard_map/dot_general | solution.py:237
  35.1 0.5 %collective-permute-done.16.refs_3_ = bf16[64,384]{1,0:T(8,128)(2,1)S(1)} collective-permute-done((bf16[64,384]{1,0:T(8,128)(2,1)S(1)}, bf16[64,384]{1,0:T(8,128)(2,1)S(1)}, u32[]{:S(2)}, u32[]{:S(2)}) %collective-permute-start.16) | collective-permute-done | bytes 49184 | tf_op jit(solution)/shard_map/ppermute | solution.py:17
  35.6 1.3 %collective-permute-done.15.refs_2_ = bf16[64,384]{1,0:T(8,128)(2,1)S(1)} collective-permute-done((bf16[64,384]{1,0:T(8,128)(2,1)S(1)}, bf16[64,384]{1,0:T(8,128)(2,1)S(1)}, u32[]{:S(2)}, u32[]{:S(2)}) %collective-permute-start.15) | collective-permute-done | bytes 49184 | tf_op jit(solution)/shard_map/ppermute | solution.py:17
  36.9 0.0 collective-permute-done.14.refs_1_
  36.9 1.2 %last_stage.1 = (bf16[64,384]{1,0:T(8,128)(2,1)}, bf16[1280,384]{1,0:T(8,128)(2,1)}) custom-call(bf16[64,384]{1,0:T(8,128)(2,1)S(1)} %product.3.refs_0_, bf16[64,384]{1,0:T(8,128)(2,1)S(1)} %collective-permute-done.14.refs_1_, bf16[64,384]{1,0:T(8,128)(2,1)S(1)} %collective-permute-done.15.refs_2_, bf16[64,384]{1,0:T(8,128)(2,1)S(1)} %collective-permute-done.16.refs_3_, ...), custom_call_target="tpu_custom_call" | custom-call | tf_op jit(solution)/shard_map/last_stage/pallas_call | solution.py:169
  (2 shorter events, 0.0 us)
Async XLA Ops:
  0.6 7.3 %collective-permute-start.2 = (bf16[16,1280]{1,0:T(8,128)(2,1)}, bf16[16,1280]{1,0:T(8,128)(2,1)S(1)}, u32[]{:S(2)}, u32[]{:S(2)}) collective-permute-start(bf16[16,1280]{1,0:T(8,128)(2,1)} %bitcast.10), channel_id=1, source_target_pairs={{0,12},{4,8},{8,4},{12,0},{1,13},{5,9},{9,5},{13,1},{2,14},{6,10},... | collective-permute-start | bytes 122888 | tf_op jit(solution)/shard_map/ppermute | solution.py:17
  5.8 5.1 %collective-permute-start.1 = (bf16[16,1280]{1,0:T(8,128)(2,1)}, bf16[16,1280]{1,0:T(8,128)(2,1)S(1)}, u32[]{:S(2)}, u32[]{:S(2)}) collective-permute-start(bf16[16,1280]{1,0:T(8,128)(2,1)} %bitcast.11), channel_id=1, source_target_pairs={{0,8},{4,12},{8,0},{12,4},{1,9},{5,13},{9,1},{13,5},{2,10},{6,14},... | collective-permute-start | bytes 122888 | tf_op jit(solution)/shard_map/ppermute | solution.py:17
  5.8 5.1 %collective-permute-start = (bf16[16,1280]{1,0:T(8,128)(2,1)}, bf16[16,1280]{1,0:T(8,128)(2,1)S(1)}, u32[]{:S(2)}, u32[]{:S(2)}) collective-permute-start(bf16[16,1280]{1,0:T(8,128)(2,1)} %bitcast.12), channel_id=1, source_target_pairs={{0,4},{4,0},{8,12},{12,8},{1,5},{5,1},{9,13},{13,9},{2,6},{6,2},{1... | collective-permute-start | bytes 122888 | tf_op jit(solution)/shard_map/ppermute | solution.py:17
  6.4 6.7 %copy-start.2 = (f32[384]{0:T(512)S(1)}, f32[384]{0:T(512)}, u32[]{:S(2)}) copy-start(f32[384]{0:T(512)} %param.8) | copy-start | bytes 4612
  6.4 9.8 %copy-start = (bf16[384,1,1280]{2,0,1:T(8,128)(2,1)S(1)}, bf16[384,1,1280]{2,0,1:T(8,128)(2,1)}, u32[]{:S(2)}) copy-start(bf16[384,1,1280]{2,0,1:T(8,128)(2,1)} %param.7) | copy-start | bytes 2949124
  6.4 9.8 %copy-start.1 = (f32[1,1280]{1,0:T(1,128)S(1)}, f32[1,1280]{1,0:T(1,128)}, u32[]{:S(2)}) copy-start(f32[1,1280]{1,0:T(1,128)} %refs_7_.1) | copy-start | bytes 15364
  11.2 4.1 %collective-permute-start.5 = (bf16[64,384]{1,0:T(8,128)(2,1)S(1)}, bf16[64,384]{1,0:T(8,128)(2,1)S(1)}, u32[]{:S(2)}, u32[]{:S(2)}) collective-permute-start(bf16[64,384]{1,0:T(8,128)(2,1)S(1)} %product.2.refs_0_), channel_id=1, source_target_pairs={{0,3},{1,2},{2,1},{3,0},{4,7},{5,6},{6,5},{7,4},{8,11},{9,10},{10,... | collective-permute-start | bytes 147464 | tf_op jit(solution)/shard_map/ppermute | solution.py:17
  11.3 4.9 %collective-permute-start.4 = (bf16[64,384]{1,0:T(8,128)(2,1)S(1)}, bf16[64,384]{1,0:T(8,128)(2,1)S(1)}, u32[]{:S(2)}, u32[]{:S(2)}) collective-permute-start(bf16[64,384]{1,0:T(8,128)(2,1)S(1)} %product.2.refs_0_), channel_id=1, source_target_pairs={{0,2},{1,3},{2,0},{3,1},{4,6},{5,7},{6,4},{7,5},{8,10},{9,11},{10,... | collective-permute-start | bytes 147464 | tf_op jit(solution)/shard_map/ppermute | solution.py:17
  12.8 3.4 %collective-permute-start.3 = (bf16[64,384]{1,0:T(8,128)(2,1)S(1)}, bf16[64,384]{1,0:T(8,128)(2,1)S(1)}, u32[]{:S(2)}, u32[]{:S(2)}) collective-permute-start(bf16[64,384]{1,0:T(8,128)(2,1)S(1)} %product.2.refs_0_), channel_id=1, source_target_pairs={{0,1},{1,0},{2,3},{3,2},{4,5},{5,4},{6,7},{7,6},{8,9},{9,8},{10,11... | collective-permute-start | bytes 147464 | tf_op jit(solution)/shard_map/ppermute | solution.py:17
  16.5 4.3 %collective-permute-start.6 = (bf16[16,1280]{1,0:T(8,128)(2,1)S(1)}, bf16[16,1280]{1,0:T(8,128)(2,1)S(1)}, u32[]{:S(2)}, u32[]{:S(2)}) collective-permute-start(bf16[16,1280]{1,0:T(8,128)(2,1)S(1)} %get-tuple-element.15), channel_id=1, source_target_pairs={{0,1},{1,0},{2,3},{3,2},{4,5},{5,4},{6,7},{7,6},{8,9},{9,8},{10,11... | collective-permute-start | bytes 122888 | tf_op jit(solution)/shard_map/ppermute | solution.py:28
  16.7 4.1 %collective-permute-start.7 = (bf16[16,1280]{1,0:T(8,128)(2,1)S(1)}, bf16[16,1280]{1,0:T(8,128)(2,1)S(1)}, u32[]{:S(2)}, u32[]{:S(2)}) collective-permute-start(bf16[16,1280]{1,0:T(8,128)(2,1)S(1)} %get-tuple-element.16), channel_id=1, source_target_pairs={{0,5},{1,4},{2,7},{3,6},{4,1},{5,0},{6,3},{7,2},{8,13},{9,12},{10,... | collective-permute-start | bytes 122888 | tf_op jit(solution)/shard_map/ppermute | solution.py:28
  16.9 4.3 %collective-permute-start.8 = (bf16[16,1280]{1,0:T(8,128)(2,1)S(1)}, bf16[16,1280]{1,0:T(8,128)(2,1)S(1)}, u32[]{:S(2)}, u32[]{:S(2)}) collective-permute-start(bf16[16,1280]{1,0:T(8,128)(2,1)S(1)} %get-tuple-element.17), channel_id=1, source_target_pairs={{0,9},{1,8},{2,11},{3,10},{4,13},{5,12},{6,15},{7,14},{8,1},{9,0},... | collective-permute-start | bytes 122888 | tf_op jit(solution)/shard_map/ppermute | solution.py:28
  18.8 5.3 %collective-permute-start.9 = (bf16[16,1280]{1,0:T(8,128)(2,1)S(1)}, bf16[16,1280]{1,0:T(8,128)(2,1)S(1)}, u32[]{:S(2)}, u32[]{:S(2)}) collective-permute-start(bf16[16,1280]{1,0:T(8,128)(2,1)S(1)} %get-tuple-element.18), channel_id=1, source_target_pairs={{0,13},{1,12},{2,15},{3,14},{4,9},{5,8},{6,11},{7,10},{8,5},{9,4},... | collective-permute-start | bytes 122888 | tf_op jit(solution)/shard_map/ppermute | solution.py:28
  24.1 5.3 %collective-permute-start.13 = (bf16[16,1280]{1,0:T(8,128)(2,1)S(1)}, bf16[16,1280]{1,0:T(8,128)(2,1)S(1)}, u32[]{:S(2)}, u32[]{:S(2)}) collective-permute-start(bf16[16,1280]{1,0:T(8,128)(2,1)S(1)} %add_convert_fusion), channel_id=1, source_target_pairs={{0,13},{1,12},{2,15},{3,14},{4,9},{5,8},{6,11},{7,10},{8,5},{9,4},... | collective-permute-start | bytes 122888 | tf_op jit(solution)/shard_map/ppermute | solution.py:28
  26.2 5.3 %collective-permute-start.12 = (bf16[16,1280]{1,0:T(8,128)(2,1)S(1)}, bf16[16,1280]{1,0:T(8,128)(2,1)S(1)}, u32[]{:S(2)}, u32[]{:S(2)}) collective-permute-start(bf16[16,1280]{1,0:T(8,128)(2,1)S(1)} %add_convert_fusion), channel_id=1, source_target_pairs={{0,9},{1,8},{2,11},{3,10},{4,13},{5,12},{6,15},{7,14},{8,1},{9,0},... | collective-permute-start | bytes 122888 | tf_op jit(solution)/shard_map/ppermute | solution.py:28
  26.2 5.3 %collective-permute-start.11 = (bf16[16,1280]{1,0:T(8,128)(2,1)S(1)}, bf16[16,1280]{1,0:T(8,128)(2,1)S(1)}, u32[]{:S(2)}, u32[]{:S(2)}) collective-permute-start(bf16[16,1280]{1,0:T(8,128)(2,1)S(1)} %add_convert_fusion), channel_id=1, source_target_pairs={{0,5},{1,4},{2,7},{3,6},{4,1},{5,0},{6,3},{7,2},{8,13},{9,12},{10,... | collective-permute-start | bytes 122888 | tf_op jit(solution)/shard_map/ppermute | solution.py:28
  28.1 3.3 %collective-permute-start.10 = (bf16[16,1280]{1,0:T(8,128)(2,1)S(1)}, bf16[16,1280]{1,0:T(8,128)(2,1)S(1)}, u32[]{:S(2)}, u32[]{:S(2)}) collective-permute-start(bf16[16,1280]{1,0:T(8,128)(2,1)S(1)} %add_convert_fusion), channel_id=1, source_target_pairs={{0,1},{1,0},{2,3},{3,2},{4,5},{5,4},{6,7},{7,6},{8,9},{9,8},{10,11... | collective-permute-start | bytes 122888 | tf_op jit(solution)/shard_map/ppermute | solution.py:28
  31.8 3.8 %collective-permute-start.16 = (bf16[64,384]{1,0:T(8,128)(2,1)S(1)}, bf16[64,384]{1,0:T(8,128)(2,1)S(1)}, u32[]{:S(2)}, u32[]{:S(2)}) collective-permute-start(bf16[64,384]{1,0:T(8,128)(2,1)S(1)} %product.3.refs_0_), channel_id=1, source_target_pairs={{0,3},{1,2},{2,1},{3,0},{4,7},{5,6},{6,5},{7,4},{8,11},{9,10},{10,... | collective-permute-start | bytes 147464 | tf_op jit(solution)/shard_map/ppermute | solution.py:17
  32.7 4.2 %collective-permute-start.15 = (bf16[64,384]{1,0:T(8,128)(2,1)S(1)}, bf16[64,384]{1,0:T(8,128)(2,1)S(1)}, u32[]{:S(2)}, u32[]{:S(2)}) collective-permute-start(bf16[64,384]{1,0:T(8,128)(2,1)S(1)} %product.3.refs_0_), channel_id=1, source_target_pairs={{0,2},{1,3},{2,0},{3,1},{4,6},{5,7},{6,4},{7,5},{8,10},{9,11},{10,... | collective-permute-start | bytes 147464 | tf_op jit(solution)/shard_map/ppermute | solution.py:17
  33.6 3.4 %collective-permute-start.14 = (bf16[64,384]{1,0:T(8,128)(2,1)S(1)}, bf16[64,384]{1,0:T(8,128)(2,1)S(1)}, u32[]{:S(2)}, u32[]{:S(2)}) collective-permute-start(bf16[64,384]{1,0:T(8,128)(2,1)S(1)} %product.3.refs_0_), channel_id=1, source_target_pairs={{0,1},{1,0},{2,3},{3,2},{4,5},{5,4},{6,7},{7,6},{8,9},{9,8},{10,11... | collective-permute-start | bytes 147464 | tf_op jit(solution)/shard_map/ppermute | solution.py:17

commit v3 on v2

--- a/solution.py
+++ b/solution.py
@@ -38,6 +38,7 @@
 HBM = pl.BlockSpec(memory_space=pltpu.HBM)
 BLOCKS = 5
 SMALL = pltpu.CompilerParams(vmem_limit_bytes=8 << 20)
+TIGHT = pltpu.CompilerParams(vmem_limit_bytes=8 << 20)
 
 
 def keep_near(*arrays):
@@ -76,7 +77,7 @@
         out_shape=jax.ShapeDtypeStruct((rows, w.shape[1]), jnp.bfloat16),
         in_specs=[VMEM] * (len(blocks) + 1),
         out_specs=VMEM,
-        compiler_params=SMALL,
+        compiler_params=TIGHT,
         name="product",
     )(*blocks, w)
 
@@ -101,7 +102,7 @@
     count, (rows, lat_dev), (row_dev, width) = len(terms), terms[0].shape, own.shape
 
     def kernel(*refs):
-        t_refs, (b_enc_ref, wd_ref, own_ref, b_dec_ref, code_ref, slope_ref), piece_refs = (
+        t_refs, (b_enc_ref, wd_ref, own_ref, b_dec_ref, code_ref, scaled_ref), piece_refs = (
             refs[:count],
             refs[count : count + 6],
             refs[count + 6 :],
@@ -112,7 +113,7 @@
         soft = jnp.maximum(x, 0.0) + jnp.log1p(small)
         code = (soft * 0.25).astype(jnp.bfloat16)
         code_ref[...] = code
-        slope_ref[...] = jnp.where(x >= 0.0, 1.0, small) / (1.0 + small)
+        scaled_ref[...] = x
         part = jnp.dot(code, wd_ref[...], preferred_element_type=jnp.float32)
         for k, ref in enumerate(piece_refs):
             piece = part[k * row_dev : (k + 1) * row_dev]
@@ -121,7 +122,7 @@
             ref[...] = piece.astype(jnp.bfloat16)
 
     pieces = rows // row_dev
-    code, slope, *parts = pl.pallas_call(
+    code, scaled, *parts = pl.pallas_call(
         kernel,
         out_shape=[
             jax.ShapeDtypeStruct((rows, lat_dev), jnp.bfloat16),
@@ -133,7 +134,7 @@
         compiler_params=SMALL,
         name="recon_pieces",
     )(*terms, b_enc, wd, own, b_dec)
-    return code, slope, parts
+    return code, scaled, parts
 
 
 def last_stage(backs, slope, acts_t, lat):
@@ -179,7 +180,7 @@
             pltpu.VMEM((depth, lat_dev), jnp.bfloat16),
             pltpu.SemaphoreType.DMA((parts + 1,)),
         ],
-        compiler_params=SMALL,
+        compiler_params=TIGHT,
         name="last_stage",
     )(*backs, slope, acts_t)
 
@@ -190,11 +191,12 @@
         blocks[0], we = keep_near(own, we)
         terms = gather_blocks(product(blocks, we), "lay", lay)
         acts_t = turned(blocks)
-        code, slope, parts = recon_pieces(terms, b_enc, wd, blocks[0], b_dec)
+        code, scaled, parts = recon_pieces(terms, b_enc, wd, blocks[0], b_dec)
         err_own = pair_sum(
             [cross(p, lat, lay, k).astype(jnp.float32) for k, p in enumerate(parts)]
         ).astype(jnp.bfloat16)
         wd_t = turned([wd])
+        slope = jax.nn.sigmoid(scaled)
         errs = [cross(err_own, lat, lay, k) for k in range(lat)]
         backs = gather_blocks(product(errs, wd_t), "lay", lay)
         lat_grad, enc_grad = last_stage(backs, slope, acts_t, lat)

time: 38.3 us -> 38.3 us (level)
  transfers between devices with their start and end apart: 17 -> 17, of which waited for: 10 -> 9; matrix products, arithmetic and copies ran while one was open for 4% -> 4% of each run, Pallas kernels for 5% -> 5%
where the time goes in v3:
time: 38.3 us; the launch traced here: 38.1 us
  starting transfers between devices  18.2 us (48%)
  waiting for transfers between devices  13.9 us (36%)
  Pallas kernels  3.87 us (10%)
  matrix products  1.4 us (4%)
  between operations  0.73 us (2%)
    ppermute x9, starting transfers between devices, swap(): return lax.ppermute(x, axis, [(a, a ^ step) for a in range(size)])  9.63 us
    ppermute x8, starting transfers between devices, cross(): return lax.ppermute(x, ('lat', 'lay'), pairs)  8.57 us
    ppermute x9, waiting for transfers between devices, swap(): return lax.ppermute(x, axis, [(a, a ^ step) for a in range(size)])  8.04 us
    ppermute x8, waiting for transfers between devices, cross(): return lax.ppermute(x, ('lat', 'lay'), pairs)  5.82 us
    dot_general x1, matrix products, on_device(): lax.dot_general(code, err, (((0,), (0,)), ((), ())), preferred_element_ty...  1.4 us
    pallas_call x1, Pallas kernels, keep_near(): pl.pallas_call(kernel, out_shape=[jax.ShapeDtypeStruct(a.shape, a.dtype)...  1.33 us
    pallas_call x1, Pallas kernels, last_stage(): pl.pallas_call(kernel, out_shape=(jax.ShapeDtypeStruct((rows, lat_dev), j...  1.2 us
  transfers between devices with their start and end apart: 17, of which 9 were waited for; matrix products, arithmetic and copies ran while one was open for 4% of the time, Pallas kernels for 5%

profile of v3, /device:TPU:0, one launch (start us, length us, event | category | flops | bytes accessed | tf_op | source)
XLA Modules:
  0.0 38.1 jit_solution(10823964166545720922)
XLA Ops:
  0.6 5.1 %collective-permute-start.2 = (bf16[16,1280]{1,0:T(8,128)(2,1)}, bf16[16,1280]{1,0:T(8,128)(2,1)S(1)}, u32[]{:S(2)}, u32[]{:S(2)}) collective-permute-start(bf16[16,1280]{1,0:T(8,128)(2,1)} %bitcast.10), channel_id=1, source_target_pairs={{0,12},{4,8},{8,4},{12,0},{1,13},{5,9},{9,5},{13,1},{2,14},{6,10},... | collective-permute-start | bytes 122888 | tf_op jit(solution)/shard_map/ppermute | solution.py:17
  5.8 0.0 collective-permute-start.1
  5.8 0.6 %collective-permute-start = (bf16[16,1280]{1,0:T(8,128)(2,1)}, bf16[16,1280]{1,0:T(8,128)(2,1)S(1)}, u32[]{:S(2)}, u32[]{:S(2)}) collective-permute-start(bf16[16,1280]{1,0:T(8,128)(2,1)} %bitcast.12), channel_id=1, source_target_pairs={{0,4},{4,0},{8,12},{12,8},{1,5},{5,1},{9,13},{13,9},{2,6},{6,2},{1... | collective-permute-start | bytes 122888 | tf_op jit(solution)/shard_map/ppermute | solution.py:17
  6.4 0.0 copy-start.2
  6.4 0.0 copy-start
  6.4 0.0 copy-start.1
  6.4 1.3 %keep_near.1 = (bf16[16,1280]{1,0:T(8,128)(2,1)S(1)}, bf16[1280,384]{1,0:T(8,128)(2,1)S(1)}) custom-call(bf16[16,1280]{1,0:T(8,128)(2,1)} %bitcast.13, bf16[1280,384]{1,0:T(8,128)(2,1)} %bitcast.9), custom_call_target="tpu_custom_call" | custom-call | tf_op jit(solution)/shard_map/keep_near/pallas_call | solution.py:57
  7.8 0.2 collective-permute-done.2.refs_3_
  8.0 2.9 %collective-permute-done.1.refs_2_ = bf16[16,1280]{1,0:T(8,128)(2,1)S(1)} collective-permute-done((bf16[16,1280]{1,0:T(8,128)(2,1)}, bf16[16,1280]{1,0:T(8,128)(2,1)S(1)}, u32[]{:S(2)}, u32[]{:S(2)}) %collective-permute-start.1) | collective-permute-done | bytes 40992 | tf_op jit(solution)/shard_map/ppermute | solution.py:17
  10.9 0.0 collective-permute-done.refs_1_
  10.9 0.3 product.2.refs_0_
  11.2 0.1 collective-permute-start.5
  11.3 1.6 %collective-permute-start.4 = (bf16[64,384]{1,0:T(8,128)(2,1)S(1)}, bf16[64,384]{1,0:T(8,128)(2,1)S(1)}, u32[]{:S(2)}, u32[]{:S(2)}) collective-permute-start(bf16[64,384]{1,0:T(8,128)(2,1)S(1)} %product.2.refs_0_), channel_id=1, source_target_pairs={{0,2},{1,3},{2,0},{3,1},{4,6},{5,7},{6,4},{7,5},{8,10},{9,11},{10,... | collective-permute-start | bytes 147464 | tf_op jit(solution)/shard_map/ppermute | solution.py:17
  12.8 0.3 collective-permute-start.3
  13.1 0.0 copy-done.2
  13.1 2.1 %collective-permute-done.5.refs_3_ = bf16[64,384]{1,0:T(8,128)(2,1)S(1)} collective-permute-done((bf16[64,384]{1,0:T(8,128)(2,1)S(1)}, bf16[64,384]{1,0:T(8,128)(2,1)S(1)}, u32[]{:S(2)}, u32[]{:S(2)}) %collective-permute-start.5) | collective-permute-done | bytes 49184 | tf_op jit(solution)/shard_map/ppermute | solution.py:17
  15.2 0.9 %collective-permute-done.4.refs_2_ = bf16[64,384]{1,0:T(8,128)(2,1)S(1)} collective-permute-done((bf16[64,384]{1,0:T(8,128)(2,1)S(1)}, bf16[64,384]{1,0:T(8,128)(2,1)S(1)}, u32[]{:S(2)}, u32[]{:S(2)}) %collective-permute-start.4) | collective-permute-done | bytes 49184 | tf_op jit(solution)/shard_map/ppermute | solution.py:17
  16.2 0.0 collective-permute-done.3.refs_1_
  16.2 0.0 copy-done
  16.2 0.0 copy-done.1
  16.2 0.3 recon_pieces.1
  16.5 0.2 collective-permute-start.6
  16.7 0.2 collective-permute-start.7
  16.9 1.9 %collective-permute-start.8 = (bf16[16,1280]{1,0:T(8,128)(2,1)S(1)}, bf16[16,1280]{1,0:T(8,128)(2,1)S(1)}, u32[]{:S(2)}, u32[]{:S(2)}) collective-permute-start(bf16[16,1280]{1,0:T(8,128)(2,1)S(1)} %get-tuple-element.17), channel_id=1, source_target_pairs={{0,9},{1,8},{2,11},{3,10},{4,13},{5,12},{6,15},{7,14},{8,1},{9,0},... | collective-permute-start | bytes 122888 | tf_op jit(solution)/shard_map/ppermute | solution.py:28
  18.7 2.1 %collective-permute-start.9 = (bf16[16,1280]{1,0:T(8,128)(2,1)S(1)}, bf16[16,1280]{1,0:T(8,128)(2,1)S(1)}, u32[]{:S(2)}, u32[]{:S(2)}) collective-permute-start(bf16[16,1280]{1,0:T(8,128)(2,1)S(1)} %get-tuple-element.18), channel_id=1, source_target_pairs={{0,13},{1,12},{2,15},{3,14},{4,9},{5,8},{6,11},{7,10},{8,5},{9,4},... | collective-permute-start | bytes 122888 | tf_op jit(solution)/shard_map/ppermute | solution.py:28
  20.8 0.3 turned.2.refs_4_
  21.1 0.1 turned.3.refs_5_
  21.3 0.0 collective-permute-done.6
  21.3 0.0 collective-permute-done.7
  21.3 0.0 collective-permute-done.8
  21.3 2.8 %collective-permute-done.9 = bf16[16,1280]{1,0:T(8,128)(2,1)S(1)} collective-permute-done((bf16[16,1280]{1,0:T(8,128)(2,1)S(1)}, bf16[16,1280]{1,0:T(8,128)(2,1)S(1)}, u32[]{:S(2)}, u32[]{:S(2)}) %collective-permute-start.9) | collective-permute-done | bytes 40992 | tf_op jit(solution)/shard_map/ppermute | solution.py:28
  24.1 2.0 %collective-permute-start.13 = (bf16[16,1280]{1,0:T(8,128)(2,1)S(1)}, bf16[16,1280]{1,0:T(8,128)(2,1)S(1)}, u32[]{:S(2)}, u32[]{:S(2)}) collective-permute-start(bf16[16,1280]{1,0:T(8,128)(2,1)S(1)} %add_convert_fusion), channel_id=1, source_target_pairs={{0,13},{1,12},{2,15},{3,14},{4,9},{5,8},{6,11},{7,10},{8,5},{9,4},... | collective-permute-start | bytes 122888 | tf_op jit(solution)/shard_map/ppermute | solution.py:28
  26.1 0.0 collective-permute-start.12
  26.1 2.0 %collective-permute-start.11 = (bf16[16,1280]{1,0:T(8,128)(2,1)S(1)}, bf16[16,1280]{1,0:T(8,128)(2,1)S(1)}, u32[]{:S(2)}, u32[]{:S(2)}) collective-permute-start(bf16[16,1280]{1,0:T(8,128)(2,1)S(1)} %add_convert_fusion), channel_id=1, source_target_pairs={{0,5},{1,4},{2,7},{3,6},{4,1},{5,0},{6,3},{7,2},{8,13},{9,12},{10,... | collective-permute-start | bytes 122888 | tf_op jit(solution)/shard_map/ppermute | solution.py:28
  28.1 0.3 collective-permute-start.10
  28.4 1.0 %collective-permute-done.13.refs_3_ = bf16[16,1280]{1,0:T(8,128)(2,1)S(1)} collective-permute-done((bf16[16,1280]{1,0:T(8,128)(2,1)S(1)}, bf16[16,1280]{1,0:T(8,128)(2,1)S(1)}, u32[]{:S(2)}, u32[]{:S(2)}) %collective-permute-start.13) | collective-permute-done | bytes 40992 | tf_op jit(solution)/shard_map/ppermute | solution.py:28
  29.4 2.0 %collective-permute-done.12.refs_2_ = bf16[16,1280]{1,0:T(8,128)(2,1)S(1)} collective-permute-done((bf16[16,1280]{1,0:T(8,128)(2,1)S(1)}, bf16[16,1280]{1,0:T(8,128)(2,1)S(1)}, u32[]{:S(2)}, u32[]{:S(2)}) %collective-permute-start.12) | collective-permute-done | bytes 40992 | tf_op jit(solution)/shard_map/ppermute | solution.py:28
  31.5 0.0 collective-permute-done.11.refs_1_
  31.5 0.0 collective-permute-done.10.refs_0_
  31.5 0.3 product.3.refs_0_
  31.8 0.9 %collective-permute-start.16 = (bf16[64,384]{1,0:T(8,128)(2,1)S(1)}, bf16[64,384]{1,0:T(8,128)(2,1)S(1)}, u32[]{:S(2)}, u32[]{:S(2)}) collective-permute-start(bf16[64,384]{1,0:T(8,128)(2,1)S(1)} %product.3.refs_0_), channel_id=1, source_target_pairs={{0,3},{1,2},{2,1},{3,0},{4,7},{5,6},{6,5},{7,4},{8,11},{9,10},{10,... | collective-permute-start | bytes 147464 | tf_op jit(solution)/shard_map/ppermute | solution.py:17
  32.7 0.9 %collective-permute-start.15 = (bf16[64,384]{1,0:T(8,128)(2,1)S(1)}, bf16[64,384]{1,0:T(8,128)(2,1)S(1)}, u32[]{:S(2)}, u32[]{:S(2)}) collective-permute-start(bf16[64,384]{1,0:T(8,128)(2,1)S(1)} %product.3.refs_0_), channel_id=1, source_target_pairs={{0,2},{1,3},{2,0},{3,1},{4,6},{5,7},{6,4},{7,5},{8,10},{9,11},{10,... | collective-permute-start | bytes 147464 | tf_op jit(solution)/shard_map/ppermute | solution.py:17
  33.6 0.1 collective-permute-start.14
  33.7 1.4 %fusion = bf16[384,1,1280]{2,0,1:T(8,128)(2,1)} fusion(bf16[64,384]{1,0:T(8,128)(2,1)S(1)} %get-tuple-element.22, bf16[16,1280]{1,0:T(8,128)(2,1)S(1)} %collective-permute-done.13.refs_3_, bf16[16,1280]{1,0:T(8,128)(2,1)S(1)} %collective-permute-done.12.refs_2_, bf16[16,1280]{1,0:T(8,128)(2,1)S(1)} %collective-permute-done.11.refs_1_, ...), kind=kOutput, calls=%fused_computation.1 | convolution fusion | flops 64061440 | bytes 1196032 | tf_op jit(solution)/shard_map/dot_general | solution.py:239
  35.1 0.5 %collective-permute-done.16.refs_3_ = bf16[64,384]{1,0:T(8,128)(2,1)S(1)} collective-permute-done((bf16[64,384]{1,0:T(8,128)(2,1)S(1)}, bf16[64,384]{1,0:T(8,128)(2,1)S(1)}, u32[]{:S(2)}, u32[]{:S(2)}) %collective-permute-start.16) | collective-permute-done | bytes 49184 | tf_op jit(solution)/shard_map/ppermute | solution.py:17
  35.6 1.3 %collective-permute-done.15.refs_2_ = bf16[64,384]{1,0:T(8,128)(2,1)S(1)} collective-permute-done((bf16[64,384]{1,0:T(8,128)(2,1)S(1)}, bf16[64,384]{1,0:T(8,128)(2,1)S(1)}, u32[]{:S(2)}, u32[]{:S(2)}) %collective-permute-start.15) | collective-permute-done | bytes 49184 | tf_op jit(solution)/shard_map/ppermute | solution.py:17
  36.9 0.0 collective-permute-done.14.refs_1_
  36.9 1.2 %last_stage.1 = (bf16[64,384]{1,0:T(8,128)(2,1)}, bf16[1280,384]{1,0:T(8,128)(2,1)}) custom-call(bf16[64,384]{1,0:T(8,128)(2,1)S(1)} %product.3.refs_0_, bf16[64,384]{1,0:T(8,128)(2,1)S(1)} %collective-permute-done.14.refs_1_, bf16[64,384]{1,0:T(8,128)(2,1)S(1)} %collective-permute-done.15.refs_2_, bf16[64,384]{1,0:T(8,128)(2,1)S(1)} %collective-permute-done.16.refs_3_, ...), custom_call_target="tpu_custom_call" | custom-call | tf_op jit(solution)/shard_map/last_stage/pallas_call | solution.py:170
  (3 shorter events, 0.1 us)
Async XLA Ops:
  0.6 7.3 %collective-permute-start.2 = (bf16[16,1280]{1,0:T(8,128)(2,1)}, bf16[16,1280]{1,0:T(8,128)(2,1)S(1)}, u32[]{:S(2)}, u32[]{:S(2)}) collective-permute-start(bf16[16,1280]{1,0:T(8,128)(2,1)} %bitcast.10), channel_id=1, source_target_pairs={{0,12},{4,8},{8,4},{12,0},{1,13},{5,9},{9,5},{13,1},{2,14},{6,10},... | collective-permute-start | bytes 122888 | tf_op jit(solution)/shard_map/ppermute | solution.py:17
  5.8 5.1 %collective-permute-start.1 = (bf16[16,1280]{1,0:T(8,128)(2,1)}, bf16[16,1280]{1,0:T(8,128)(2,1)S(1)}, u32[]{:S(2)}, u32[]{:S(2)}) collective-permute-start(bf16[16,1280]{1,0:T(8,128)(2,1)} %bitcast.11), channel_id=1, source_target_pairs={{0,8},{4,12},{8,0},{12,4},{1,9},{5,13},{9,1},{13,5},{2,10},{6,14},... | collective-permute-start | bytes 122888 | tf_op jit(solution)/shard_map/ppermute | solution.py:17
  5.8 5.1 %collective-permute-start = (bf16[16,1280]{1,0:T(8,128)(2,1)}, bf16[16,1280]{1,0:T(8,128)(2,1)S(1)}, u32[]{:S(2)}, u32[]{:S(2)}) collective-permute-start(bf16[16,1280]{1,0:T(8,128)(2,1)} %bitcast.12), channel_id=1, source_target_pairs={{0,4},{4,0},{8,12},{12,8},{1,5},{5,1},{9,13},{13,9},{2,6},{6,2},{1... | collective-permute-start | bytes 122888 | tf_op jit(solution)/shard_map/ppermute | solution.py:17
  6.4 6.7 %copy-start.2 = (f32[384]{0:T(512)S(1)}, f32[384]{0:T(512)}, u32[]{:S(2)}) copy-start(f32[384]{0:T(512)} %param.8) | copy-start | bytes 4612
  6.4 9.8 %copy-start = (bf16[384,1,1280]{2,0,1:T(8,128)(2,1)S(1)}, bf16[384,1,1280]{2,0,1:T(8,128)(2,1)}, u32[]{:S(2)}) copy-start(bf16[384,1,1280]{2,0,1:T(8,128)(2,1)} %param.7) | copy-start | bytes 2949124
  6.4 9.8 %copy-start.1 = (f32[1,1280]{1,0:T(1,128)S(1)}, f32[1,1280]{1,0:T(1,128)}, u32[]{:S(2)}) copy-start(f32[1,1280]{1,0:T(1,128)} %refs_7_.1) | copy-start | bytes 15364
  11.2 4.1 %collective-permute-start.5 = (bf16[64,384]{1,0:T(8,128)(2,1)S(1)}, bf16[64,384]{1,0:T(8,128)(2,1)S(1)}, u32[]{:S(2)}, u32[]{:S(2)}) collective-permute-start(bf16[64,384]{1,0:T(8,128)(2,1)S(1)} %product.2.refs_0_), channel_id=1, source_target_pairs={{0,3},{1,2},{2,1},{3,0},{4,7},{5,6},{6,5},{7,4},{8,11},{9,10},{10,... | collective-permute-start | bytes 147464 | tf_op jit(solution)/shard_map/ppermute | solution.py:17
  11.3 4.9 %collective-permute-start.4 = (bf16[64,384]{1,0:T(8,128)(2,1)S(1)}, bf16[64,384]{1,0:T(8,128)(2,1)S(1)}, u32[]{:S(2)}, u32[]{:S(2)}) collective-permute-start(bf16[64,384]{1,0:T(8,128)(2,1)S(1)} %product.2.refs_0_), channel_id=1, source_target_pairs={{0,2},{1,3},{2,0},{3,1},{4,6},{5,7},{6,4},{7,5},{8,10},{9,11},{10,... | collective-permute-start | bytes 147464 | tf_op jit(solution)/shard_map/ppermute | solution.py:17
  12.8 3.4 %collective-permute-start.3 = (bf16[64,384]{1,0:T(8,128)(2,1)S(1)}, bf16[64,384]{1,0:T(8,128)(2,1)S(1)}, u32[]{:S(2)}, u32[]{:S(2)}) collective-permute-start(bf16[64,384]{1,0:T(8,128)(2,1)S(1)} %product.2.refs_0_), channel_id=1, source_target_pairs={{0,1},{1,0},{2,3},{3,2},{4,5},{5,4},{6,7},{7,6},{8,9},{9,8},{10,11... | collective-permute-start | bytes 147464 | tf_op jit(solution)/shard_map/ppermute | solution.py:17
  16.5 4.8 %collective-permute-start.6 = (bf16[16,1280]{1,0:T(8,128)(2,1)S(1)}, bf16[16,1280]{1,0:T(8,128)(2,1)S(1)}, u32[]{:S(2)}, u32[]{:S(2)}) collective-permute-start(bf16[16,1280]{1,0:T(8,128)(2,1)S(1)} %get-tuple-element.15), channel_id=1, source_target_pairs={{0,1},{1,0},{2,3},{3,2},{4,5},{5,4},{6,7},{7,6},{8,9},{9,8},{10,11... | collective-permute-start | bytes 122888 | tf_op jit(solution)/shard_map/ppermute | solution.py:28
  16.7 4.6 %collective-permute-start.7 = (bf16[16,1280]{1,0:T(8,128)(2,1)S(1)}, bf16[16,1280]{1,0:T(8,128)(2,1)S(1)}, u32[]{:S(2)}, u32[]{:S(2)}) collective-permute-start(bf16[16,1280]{1,0:T(8,128)(2,1)S(1)} %get-tuple-element.16), channel_id=1, source_target_pairs={{0,5},{1,4},{2,7},{3,6},{4,1},{5,0},{6,3},{7,2},{8,13},{9,12},{10,... | collective-permute-start | bytes 122888 | tf_op jit(solution)/shard_map/ppermute | solution.py:28
  16.9 4.4 %collective-permute-start.8 = (bf16[16,1280]{1,0:T(8,128)(2,1)S(1)}, bf16[16,1280]{1,0:T(8,128)(2,1)S(1)}, u32[]{:S(2)}, u32[]{:S(2)}) collective-permute-start(bf16[16,1280]{1,0:T(8,128)(2,1)S(1)} %get-tuple-element.17), channel_id=1, source_target_pairs={{0,9},{1,8},{2,11},{3,10},{4,13},{5,12},{6,15},{7,14},{8,1},{9,0},... | collective-permute-start | bytes 122888 | tf_op jit(solution)/shard_map/ppermute | solution.py:28
  18.7 5.4 %collective-permute-start.9 = (bf16[16,1280]{1,0:T(8,128)(2,1)S(1)}, bf16[16,1280]{1,0:T(8,128)(2,1)S(1)}, u32[]{:S(2)}, u32[]{:S(2)}) collective-permute-start(bf16[16,1280]{1,0:T(8,128)(2,1)S(1)} %get-tuple-element.18), channel_id=1, source_target_pairs={{0,13},{1,12},{2,15},{3,14},{4,9},{5,8},{6,11},{7,10},{8,5},{9,4},... | collective-permute-start | bytes 122888 | tf_op jit(solution)/shard_map/ppermute | solution.py:28
  24.1 5.3 %collective-permute-start.13 = (bf16[16,1280]{1,0:T(8,128)(2,1)S(1)}, bf16[16,1280]{1,0:T(8,128)(2,1)S(1)}, u32[]{:S(2)}, u32[]{:S(2)}) collective-permute-start(bf16[16,1280]{1,0:T(8,128)(2,1)S(1)} %add_convert_fusion), channel_id=1, source_target_pairs={{0,13},{1,12},{2,15},{3,14},{4,9},{5,8},{6,11},{7,10},{8,5},{9,4},... | collective-permute-start | bytes 122888 | tf_op jit(solution)/shard_map/ppermute | solution.py:28
  26.1 5.3 %collective-permute-start.12 = (bf16[16,1280]{1,0:T(8,128)(2,1)S(1)}, bf16[16,1280]{1,0:T(8,128)(2,1)S(1)}, u32[]{:S(2)}, u32[]{:S(2)}) collective-permute-start(bf16[16,1280]{1,0:T(8,128)(2,1)S(1)} %add_convert_fusion), channel_id=1, source_target_pairs={{0,9},{1,8},{2,11},{3,10},{4,13},{5,12},{6,15},{7,14},{8,1},{9,0},... | collective-permute-start | bytes 122888 | tf_op jit(solution)/shard_map/ppermute | solution.py:28
  26.1 5.3 %collective-permute-start.11 = (bf16[16,1280]{1,0:T(8,128)(2,1)S(1)}, bf16[16,1280]{1,0:T(8,128)(2,1)S(1)}, u32[]{:S(2)}, u32[]{:S(2)}) collective-permute-start(bf16[16,1280]{1,0:T(8,128)(2,1)S(1)} %add_convert_fusion), channel_id=1, source_target_pairs={{0,5},{1,4},{2,7},{3,6},{4,1},{5,0},{6,3},{7,2},{8,13},{9,12},{10,... | collective-permute-start | bytes 122888 | tf_op jit(solution)/shard_map/ppermute | solution.py:28
  28.1 3.3 %collective-permute-start.10 = (bf16[16,1280]{1,0:T(8,128)(2,1)S(1)}, bf16[16,1280]{1,0:T(8,128)(2,1)S(1)}, u32[]{:S(2)}, u32[]{:S(2)}) collective-permute-start(bf16[16,1280]{1,0:T(8,128)(2,1)S(1)} %add_convert_fusion), channel_id=1, source_target_pairs={{0,1},{1,0},{2,3},{3,2},{4,5},{5,4},{6,7},{7,6},{8,9},{9,8},{10,11... | collective-permute-start | bytes 122888 | tf_op jit(solution)/shard_map/ppermute | solution.py:28
  31.8 3.8 %collective-permute-start.16 = (bf16[64,384]{1,0:T(8,128)(2,1)S(1)}, bf16[64,384]{1,0:T(8,128)(2,1)S(1)}, u32[]{:S(2)}, u32[]{:S(2)}) collective-permute-start(bf16[64,384]{1,0:T(8,128)(2,1)S(1)} %product.3.refs_0_), channel_id=1, source_target_pairs={{0,3},{1,2},{2,1},{3,0},{4,7},{5,6},{6,5},{7,4},{8,11},{9,10},{10,... | collective-permute-start | bytes 147464 | tf_op jit(solution)/shard_map/ppermute | solution.py:17
  32.7 4.2 %collective-permute-start.15 = (bf16[64,384]{1,0:T(8,128)(2,1)S(1)}, bf16[64,384]{1,0:T(8,128)(2,1)S(1)}, u32[]{:S(2)}, u32[]{:S(2)}) collective-permute-start(bf16[64,384]{1,0:T(8,128)(2,1)S(1)} %product.3.refs_0_), channel_id=1, source_target_pairs={{0,2},{1,3},{2,0},{3,1},{4,6},{5,7},{6,4},{7,5},{8,10},{9,11},{10,... | collective-permute-start | bytes 147464 | tf_op jit(solution)/shard_map/ppermute | solution.py:17
  33.6 3.4 %collective-permute-start.14 = (bf16[64,384]{1,0:T(8,128)(2,1)S(1)}, bf16[64,384]{1,0:T(8,128)(2,1)S(1)}, u32[]{:S(2)}, u32[]{:S(2)}) collective-permute-start(bf16[64,384]{1,0:T(8,128)(2,1)S(1)} %product.3.refs_0_), channel_id=1, source_target_pairs={{0,1},{1,0},{2,3},{3,2},{4,5},{5,4},{6,7},{7,6},{8,9},{9,8},{10,11... | collective-permute-start | bytes 147464 | tf_op jit(solution)/shard_map/ppermute | solution.py:17

commit v4 on v3

--- a/solution.py
+++ b/solution.py
@@ -36,7 +36,7 @@
 
 VMEM = pl.BlockSpec(memory_space=pltpu.VMEM)
 HBM = pl.BlockSpec(memory_space=pltpu.HBM)
-BLOCKS = 5
+BLOCKS = (1, 3, 3, 2, 1)
 SMALL = pltpu.CompilerParams(vmem_limit_bytes=8 << 20)
 TIGHT = pltpu.CompilerParams(vmem_limit_bytes=8 << 20)
 
@@ -140,8 +140,8 @@
 def last_stage(backs, slope, acts_t, lat):
     rows, lat_dev = slope.shape
     row_dev, depth = rows // lat, acts_t.shape[0]
-    parts = BLOCKS if depth % (16 * BLOCKS) == 0 else 1
-    step = depth // parts
+    shares = BLOCKS if depth % (16 * sum(BLOCKS)) == 0 else (1,)
+    parts, unit = len(shares), depth // sum(shares)
     count = len(backs)
 
     def kernel(*refs):
@@ -158,7 +158,7 @@
         copies = [pltpu.make_async_copy(grad_held, grad_ref, sems.at[parts])]
         copies[0].start()
         for n in range(parts):
-            part = pl.ds(n * step, step)
+            part = pl.ds(sum(shares[:n]) * unit, shares[n] * unit)
             held[part, :] = jnp.dot(
                 x_ref[part, :], grad, preferred_element_type=jnp.float32
             ).astype(held.dtype)

time: 38.3 us -> 38.3 us (level)
  no operation moved by 1% of the time
where the time goes in v4:
time: 38.3 us; the launch traced here: 38.2 us
  starting transfers between devices  18.2 us (48%)
  waiting for transfers between devices  13.9 us (36%)
  Pallas kernels  3.91 us (10%)
  matrix products  1.4 us (4%)
  between operations  0.73 us (2%)
    ppermute x9, starting transfers between devices, swap(): return lax.ppermute(x, axis, [(a, a ^ step) for a in range(size)])  9.63 us
    ppermute x8, starting transfers between devices, cross(): return lax.ppermute(x, ('lat', 'lay'), pairs)  8.57 us
    ppermute x9, waiting for transfers between devices, swap(): return lax.ppermute(x, axis, [(a, a ^ step) for a in range(size)])  8.04 us
    ppermute x8, waiting for transfers between devices, cross(): return lax.ppermute(x, ('lat', 'lay'), pairs)  5.82 us
    dot_general x1, matrix products, on_device(): lax.dot_general(code, err, (((0,), (0,)), ((), ())), preferred_element_ty...  1.4 us
    pallas_call x1, Pallas kernels, keep_near(): pl.pallas_call(kernel, out_shape=[jax.ShapeDtypeStruct(a.shape, a.dtype)...  1.33 us
    pallas_call x1, Pallas kernels, last_stage(): pl.pallas_call(kernel, out_shape=(jax.ShapeDtypeStruct((rows, lat_dev), j...  1.23 us
  transfers between devices with their start and end apart: 17, of which 9 were waited for; matrix products, arithmetic and copies ran while one was open for 4% of the time, Pallas kernels for 5%

profile of v4, /device:TPU:0, one launch (start us, length us, event | category | flops | bytes accessed | tf_op | source)
XLA Modules:
  0.0 38.2 jit_solution(4161588847367606573)
XLA Ops:
  0.6 5.1 %collective-permute-start.2 = (bf16[16,1280]{1,0:T(8,128)(2,1)}, bf16[16,1280]{1,0:T(8,128)(2,1)S(1)}, u32[]{:S(2)}, u32[]{:S(2)}) collective-permute-start(bf16[16,1280]{1,0:T(8,128)(2,1)} %bitcast.10), channel_id=1, source_target_pairs={{0,12},{4,8},{8,4},{12,0},{1,13},{5,9},{9,5},{13,1},{2,14},{6,10},... | collective-permute-start | bytes 122888 | tf_op jit(solution)/shard_map/ppermute | solution.py:17
  5.8 0.0 collective-permute-start.1
  5.8 0.6 %collective-permute-start = (bf16[16,1280]{1,0:T(8,128)(2,1)}, bf16[16,1280]{1,0:T(8,128)(2,1)S(1)}, u32[]{:S(2)}, u32[]{:S(2)}) collective-permute-start(bf16[16,1280]{1,0:T(8,128)(2,1)} %bitcast.12), channel_id=1, source_target_pairs={{0,4},{4,0},{8,12},{12,8},{1,5},{5,1},{9,13},{13,9},{2,6},{6,2},{1... | collective-permute-start | bytes 122888 | tf_op jit(solution)/shard_map/ppermute | solution.py:17
  6.4 0.0 copy-start.2
  6.4 0.0 copy-start
  6.4 0.0 copy-start.1
  6.4 1.3 %keep_near.1 = (bf16[16,1280]{1,0:T(8,128)(2,1)S(1)}, bf16[1280,384]{1,0:T(8,128)(2,1)S(1)}) custom-call(bf16[16,1280]{1,0:T(8,128)(2,1)} %bitcast.13, bf16[1280,384]{1,0:T(8,128)(2,1)} %bitcast.9), custom_call_target="tpu_custom_call" | custom-call | tf_op jit(solution)/shard_map/keep_near/pallas_call | solution.py:57
  7.8 0.2 collective-permute-done.2.refs_3_
  8.0 2.9 %collective-permute-done.1.refs_2_ = bf16[16,1280]{1,0:T(8,128)(2,1)S(1)} collective-permute-done((bf16[16,1280]{1,0:T(8,128)(2,1)}, bf16[16,1280]{1,0:T(8,128)(2,1)S(1)}, u32[]{:S(2)}, u32[]{:S(2)}) %collective-permute-start.1) | collective-permute-done | bytes 40992 | tf_op jit(solution)/shard_map/ppermute | solution.py:17
  10.9 0.0 collective-permute-done.refs_1_
  10.9 0.3 product.2.refs_0_
  11.2 0.1 collective-permute-start.5
  11.3 1.6 %collective-permute-start.4 = (bf16[64,384]{1,0:T(8,128)(2,1)S(1)}, bf16[64,384]{1,0:T(8,128)(2,1)S(1)}, u32[]{:S(2)}, u32[]{:S(2)}) collective-permute-start(bf16[64,384]{1,0:T(8,128)(2,1)S(1)} %product.2.refs_0_), channel_id=1, source_target_pairs={{0,2},{1,3},{2,0},{3,1},{4,6},{5,7},{6,4},{7,5},{8,10},{9,11},{10,... | collective-permute-start | bytes 147464 | tf_op jit(solution)/shard_map/ppermute | solution.py:17
  12.8 0.3 collective-permute-start.3
  13.1 0.0 copy-done.2
  13.1 2.1 %collective-permute-done.5.refs_3_ = bf16[64,384]{1,0:T(8,128)(2,1)S(1)} collective-permute-done((bf16[64,384]{1,0:T(8,128)(2,1)S(1)}, bf16[64,384]{1,0:T(8,128)(2,1)S(1)}, u32[]{:S(2)}, u32[]{:S(2)}) %collective-permute-start.5) | collective-permute-done | bytes 49184 | tf_op jit(solution)/shard_map/ppermute | solution.py:17
  15.2 0.9 %collective-permute-done.4.refs_2_ = bf16[64,384]{1,0:T(8,128)(2,1)S(1)} collective-permute-done((bf16[64,384]{1,0:T(8,128)(2,1)S(1)}, bf16[64,384]{1,0:T(8,128)(2,1)S(1)}, u32[]{:S(2)}, u32[]{:S(2)}) %collective-permute-start.4) | collective-permute-done | bytes 49184 | tf_op jit(solution)/shard_map/ppermute | solution.py:17
  16.2 0.0 collective-permute-done.3.refs_1_
  16.2 0.0 copy-done
  16.2 0.0 copy-done.1
  16.2 0.3 recon_pieces.1
  16.5 0.2 collective-permute-start.6
  16.7 0.2 collective-permute-start.7
  16.9 1.9 %collective-permute-start.8 = (bf16[16,1280]{1,0:T(8,128)(2,1)S(1)}, bf16[16,1280]{1,0:T(8,128)(2,1)S(1)}, u32[]{:S(2)}, u32[]{:S(2)}) collective-permute-start(bf16[16,1280]{1,0:T(8,128)(2,1)S(1)} %get-tuple-element.17), channel_id=1, source_target_pairs={{0,9},{1,8},{2,11},{3,10},{4,13},{5,12},{6,15},{7,14},{8,1},{9,0},... | collective-permute-start | bytes 122888 | tf_op jit(solution)/shard_map/ppermute | solution.py:28
  18.7 2.1 %collective-permute-start.9 = (bf16[16,1280]{1,0:T(8,128)(2,1)S(1)}, bf16[16,1280]{1,0:T(8,128)(2,1)S(1)}, u32[]{:S(2)}, u32[]{:S(2)}) collective-permute-start(bf16[16,1280]{1,0:T(8,128)(2,1)S(1)} %get-tuple-element.18), channel_id=1, source_target_pairs={{0,13},{1,12},{2,15},{3,14},{4,9},{5,8},{6,11},{7,10},{8,5},{9,4},... | collective-permute-start | bytes 122888 | tf_op jit(solution)/shard_map/ppermute | solution.py:28
  20.8 0.3 turned.2.refs_4_
  21.1 0.1 turned.3.refs_5_
  21.3 0.0 collective-permute-done.6
  21.3 0.0 collective-permute-done.7
  21.3 0.0 collective-permute-done.8
  21.3 2.8 %collective-permute-done.9 = bf16[16,1280]{1,0:T(8,128)(2,1)S(1)} collective-permute-done((bf16[16,1280]{1,0:T(8,128)(2,1)S(1)}, bf16[16,1280]{1,0:T(8,128)(2,1)S(1)}, u32[]{:S(2)}, u32[]{:S(2)}) %collective-permute-start.9) | collective-permute-done | bytes 40992 | tf_op jit(solution)/shard_map/ppermute | solution.py:28
  24.1 2.0 %collective-permute-start.13 = (bf16[16,1280]{1,0:T(8,128)(2,1)S(1)}, bf16[16,1280]{1,0:T(8,128)(2,1)S(1)}, u32[]{:S(2)}, u32[]{:S(2)}) collective-permute-start(bf16[16,1280]{1,0:T(8,128)(2,1)S(1)} %add_convert_fusion), channel_id=1, source_target_pairs={{0,13},{1,12},{2,15},{3,14},{4,9},{5,8},{6,11},{7,10},{8,5},{9,4},... | collective-permute-start | bytes 122888 | tf_op jit(solution)/shard_map/ppermute | solution.py:28
  26.1 0.0 collective-permute-start.12
  26.1 2.0 %collective-permute-start.11 = (bf16[16,1280]{1,0:T(8,128)(2,1)S(1)}, bf16[16,1280]{1,0:T(8,128)(2,1)S(1)}, u32[]{:S(2)}, u32[]{:S(2)}) collective-permute-start(bf16[16,1280]{1,0:T(8,128)(2,1)S(1)} %add_convert_fusion), channel_id=1, source_target_pairs={{0,5},{1,4},{2,7},{3,6},{4,1},{5,0},{6,3},{7,2},{8,13},{9,12},{10,... | collective-permute-start | bytes 122888 | tf_op jit(solution)/shard_map/ppermute | solution.py:28
  28.1 0.3 collective-permute-start.10
  28.4 1.0 %collective-permute-done.13.refs_3_ = bf16[16,1280]{1,0:T(8,128)(2,1)S(1)} collective-permute-done((bf16[16,1280]{1,0:T(8,128)(2,1)S(1)}, bf16[16,1280]{1,0:T(8,128)(2,1)S(1)}, u32[]{:S(2)}, u32[]{:S(2)}) %collective-permute-start.13) | collective-permute-done | bytes 40992 | tf_op jit(solution)/shard_map/ppermute | solution.py:28
  29.4 2.0 %collective-permute-done.12.refs_2_ = bf16[16,1280]{1,0:T(8,128)(2,1)S(1)} collective-permute-done((bf16[16,1280]{1,0:T(8,128)(2,1)S(1)}, bf16[16,1280]{1,0:T(8,128)(2,1)S(1)}, u32[]{:S(2)}, u32[]{:S(2)}) %collective-permute-start.12) | collective-permute-done | bytes 40992 | tf_op jit(solution)/shard_map/ppermute | solution.py:28
  31.5 0.0 collective-permute-done.11.refs_1_
  31.5 0.0 collective-permute-done.10.refs_0_
  31.5 0.3 product.3.refs_0_
  31.8 0.9 %collective-permute-start.16 = (bf16[64,384]{1,0:T(8,128)(2,1)S(1)}, bf16[64,384]{1,0:T(8,128)(2,1)S(1)}, u32[]{:S(2)}, u32[]{:S(2)}) collective-permute-start(bf16[64,384]{1,0:T(8,128)(2,1)S(1)} %product.3.refs_0_), channel_id=1, source_target_pairs={{0,3},{1,2},{2,1},{3,0},{4,7},{5,6},{6,5},{7,4},{8,11},{9,10},{10,... | collective-permute-start | bytes 147464 | tf_op jit(solution)/shard_map/ppermute | solution.py:17
  32.7 0.9 %collective-permute-start.15 = (bf16[64,384]{1,0:T(8,128)(2,1)S(1)}, bf16[64,384]{1,0:T(8,128)(2,1)S(1)}, u32[]{:S(2)}, u32[]{:S(2)}) collective-permute-start(bf16[64,384]{1,0:T(8,128)(2,1)S(1)} %product.3.refs_0_), channel_id=1, source_target_pairs={{0,2},{1,3},{2,0},{3,1},{4,6},{5,7},{6,4},{7,5},{8,10},{9,11},{10,... | collective-permute-start | bytes 147464 | tf_op jit(solution)/shard_map/ppermute | solution.py:17
  33.6 0.1 collective-permute-start.14
  33.7 1.4 %fusion = bf16[384,1,1280]{2,0,1:T(8,128)(2,1)} fusion(bf16[64,384]{1,0:T(8,128)(2,1)S(1)} %get-tuple-element.22, bf16[16,1280]{1,0:T(8,128)(2,1)S(1)} %collective-permute-done.13.refs_3_, bf16[16,1280]{1,0:T(8,128)(2,1)S(1)} %collective-permute-done.12.refs_2_, bf16[16,1280]{1,0:T(8,128)(2,1)S(1)} %collective-permute-done.11.refs_1_, ...), kind=kOutput, calls=%fused_computation.1 | convolution fusion | flops 64061440 | bytes 1196032 | tf_op jit(solution)/shard_map/dot_general | solution.py:239
  35.1 0.5 %collective-permute-done.16.refs_3_ = bf16[64,384]{1,0:T(8,128)(2,1)S(1)} collective-permute-done((bf16[64,384]{1,0:T(8,128)(2,1)S(1)}, bf16[64,384]{1,0:T(8,128)(2,1)S(1)}, u32[]{:S(2)}, u32[]{:S(2)}) %collective-permute-start.16) | collective-permute-done | bytes 49184 | tf_op jit(solution)/shard_map/ppermute | solution.py:17
  35.6 1.3 %collective-permute-done.15.refs_2_ = bf16[64,384]{1,0:T(8,128)(2,1)S(1)} collective-permute-done((bf16[64,384]{1,0:T(8,128)(2,1)S(1)}, bf16[64,384]{1,0:T(8,128)(2,1)S(1)}, u32[]{:S(2)}, u32[]{:S(2)}) %collective-permute-start.15) | collective-permute-done | bytes 49184 | tf_op jit(solution)/shard_map/ppermute | solution.py:17
  36.9 0.0 collective-permute-done.14.refs_1_
  36.9 1.2 %last_stage.1 = (bf16[64,384]{1,0:T(8,128)(2,1)}, bf16[1280,384]{1,0:T(8,128)(2,1)}) custom-call(bf16[64,384]{1,0:T(8,128)(2,1)S(1)} %product.3.refs_0_, bf16[64,384]{1,0:T(8,128)(2,1)S(1)} %collective-permute-done.14.refs_1_, bf16[64,384]{1,0:T(8,128)(2,1)S(1)} %collective-permute-done.15.refs_2_, bf16[64,384]{1,0:T(8,128)(2,1)S(1)} %collective-permute-done.16.refs_3_, ...), custom_call_target="tpu_custom_call" | custom-call | tf_op jit(solution)/shard_map/last_stage/pallas_call | solution.py:170
  (3 shorter events, 0.1 us)
Async XLA Ops:
  0.6 7.3 %collective-permute-start.2 = (bf16[16,1280]{1,0:T(8,128)(2,1)}, bf16[16,1280]{1,0:T(8,128)(2,1)S(1)}, u32[]{:S(2)}, u32[]{:S(2)}) collective-permute-start(bf16[16,1280]{1,0:T(8,128)(2,1)} %bitcast.10), channel_id=1, source_target_pairs={{0,12},{4,8},{8,4},{12,0},{1,13},{5,9},{9,5},{13,1},{2,14},{6,10},... | collective-permute-start | bytes 122888 | tf_op jit(solution)/shard_map/ppermute | solution.py:17
  5.8 5.1 %collective-permute-start.1 = (bf16[16,1280]{1,0:T(8,128)(2,1)}, bf16[16,1280]{1,0:T(8,128)(2,1)S(1)}, u32[]{:S(2)}, u32[]{:S(2)}) collective-permute-start(bf16[16,1280]{1,0:T(8,128)(2,1)} %bitcast.11), channel_id=1, source_target_pairs={{0,8},{4,12},{8,0},{12,4},{1,9},{5,13},{9,1},{13,5},{2,10},{6,14},... | collective-permute-start | bytes 122888 | tf_op jit(solution)/shard_map/ppermute | solution.py:17
  5.8 5.1 %collective-permute-start = (bf16[16,1280]{1,0:T(8,128)(2,1)}, bf16[16,1280]{1,0:T(8,128)(2,1)S(1)}, u32[]{:S(2)}, u32[]{:S(2)}) collective-permute-start(bf16[16,1280]{1,0:T(8,128)(2,1)} %bitcast.12), channel_id=1, source_target_pairs={{0,4},{4,0},{8,12},{12,8},{1,5},{5,1},{9,13},{13,9},{2,6},{6,2},{1... | collective-permute-start | bytes 122888 | tf_op jit(solution)/shard_map/ppermute | solution.py:17
  6.4 6.7 %copy-start.2 = (f32[384]{0:T(512)S(1)}, f32[384]{0:T(512)}, u32[]{:S(2)}) copy-start(f32[384]{0:T(512)} %param.8) | copy-start | bytes 4612
  6.4 9.8 %copy-start = (bf16[384,1,1280]{2,0,1:T(8,128)(2,1)S(1)}, bf16[384,1,1280]{2,0,1:T(8,128)(2,1)}, u32[]{:S(2)}) copy-start(bf16[384,1,1280]{2,0,1:T(8,128)(2,1)} %param.7) | copy-start | bytes 2949124
  6.4 9.8 %copy-start.1 = (f32[1,1280]{1,0:T(1,128)S(1)}, f32[1,1280]{1,0:T(1,128)}, u32[]{:S(2)}) copy-start(f32[1,1280]{1,0:T(1,128)} %refs_7_.1) | copy-start | bytes 15364
  11.2 4.1 %collective-permute-start.5 = (bf16[64,384]{1,0:T(8,128)(2,1)S(1)}, bf16[64,384]{1,0:T(8,128)(2,1)S(1)}, u32[]{:S(2)}, u32[]{:S(2)}) collective-permute-start(bf16[64,384]{1,0:T(8,128)(2,1)S(1)} %product.2.refs_0_), channel_id=1, source_target_pairs={{0,3},{1,2},{2,1},{3,0},{4,7},{5,6},{6,5},{7,4},{8,11},{9,10},{10,... | collective-permute-start | bytes 147464 | tf_op jit(solution)/shard_map/ppermute | solution.py:17
  11.3 4.9 %collective-permute-start.4 = (bf16[64,384]{1,0:T(8,128)(2,1)S(1)}, bf16[64,384]{1,0:T(8,128)(2,1)S(1)}, u32[]{:S(2)}, u32[]{:S(2)}) collective-permute-start(bf16[64,384]{1,0:T(8,128)(2,1)S(1)} %product.2.refs_0_), channel_id=1, source_target_pairs={{0,2},{1,3},{2,0},{3,1},{4,6},{5,7},{6,4},{7,5},{8,10},{9,11},{10,... | collective-permute-start | bytes 147464 | tf_op jit(solution)/shard_map/ppermute | solution.py:17
  12.8 3.4 %collective-permute-start.3 = (bf16[64,384]{1,0:T(8,128)(2,1)S(1)}, bf16[64,384]{1,0:T(8,128)(2,1)S(1)}, u32[]{:S(2)}, u32[]{:S(2)}) collective-permute-start(bf16[64,384]{1,0:T(8,128)(2,1)S(1)} %product.2.refs_0_), channel_id=1, source_target_pairs={{0,1},{1,0},{2,3},{3,2},{4,5},{5,4},{6,7},{7,6},{8,9},{9,8},{10,11... | collective-permute-start | bytes 147464 | tf_op jit(solution)/shard_map/ppermute | solution.py:17
  16.5 4.8 %collective-permute-start.6 = (bf16[16,1280]{1,0:T(8,128)(2,1)S(1)}, bf16[16,1280]{1,0:T(8,128)(2,1)S(1)}, u32[]{:S(2)}, u32[]{:S(2)}) collective-permute-start(bf16[16,1280]{1,0:T(8,128)(2,1)S(1)} %get-tuple-element.15), channel_id=1, source_target_pairs={{0,1},{1,0},{2,3},{3,2},{4,5},{5,4},{6,7},{7,6},{8,9},{9,8},{10,11... | collective-permute-start | bytes 122888 | tf_op jit(solution)/shard_map/ppermute | solution.py:28
  16.7 4.6 %collective-permute-start.7 = (bf16[16,1280]{1,0:T(8,128)(2,1)S(1)}, bf16[16,1280]{1,0:T(8,128)(2,1)S(1)}, u32[]{:S(2)}, u32[]{:S(2)}) collective-permute-start(bf16[16,1280]{1,0:T(8,128)(2,1)S(1)} %get-tuple-element.16), channel_id=1, source_target_pairs={{0,5},{1,4},{2,7},{3,6},{4,1},{5,0},{6,3},{7,2},{8,13},{9,12},{10,... | collective-permute-start | bytes 122888 | tf_op jit(solution)/shard_map/ppermute | solution.py:28
  16.9 4.4 %collective-permute-start.8 = (bf16[16,1280]{1,0:T(8,128)(2,1)S(1)}, bf16[16,1280]{1,0:T(8,128)(2,1)S(1)}, u32[]{:S(2)}, u32[]{:S(2)}) collective-permute-start(bf16[16,1280]{1,0:T(8,128)(2,1)S(1)} %get-tuple-element.17), channel_id=1, source_target_pairs={{0,9},{1,8},{2,11},{3,10},{4,13},{5,12},{6,15},{7,14},{8,1},{9,0},... | collective-permute-start | bytes 122888 | tf_op jit(solution)/shard_map/ppermute | solution.py:28
  18.7 5.4 %collective-permute-start.9 = (bf16[16,1280]{1,0:T(8,128)(2,1)S(1)}, bf16[16,1280]{1,0:T(8,128)(2,1)S(1)}, u32[]{:S(2)}, u32[]{:S(2)}) collective-permute-start(bf16[16,1280]{1,0:T(8,128)(2,1)S(1)} %get-tuple-element.18), channel_id=1, source_target_pairs={{0,13},{1,12},{2,15},{3,14},{4,9},{5,8},{6,11},{7,10},{8,5},{9,4},... | collective-permute-start | bytes 122888 | tf_op jit(solution)/shard_map/ppermute | solution.py:28
  24.1 5.3 %collective-permute-start.13 = (bf16[16,1280]{1,0:T(8,128)(2,1)S(1)}, bf16[16,1280]{1,0:T(8,128)(2,1)S(1)}, u32[]{:S(2)}, u32[]{:S(2)}) collective-permute-start(bf16[16,1280]{1,0:T(8,128)(2,1)S(1)} %add_convert_fusion), channel_id=1, source_target_pairs={{0,13},{1,12},{2,15},{3,14},{4,9},{5,8},{6,11},{7,10},{8,5},{9,4},... | collective-permute-start | bytes 122888 | tf_op jit(solution)/shard_map/ppermute | solution.py:28
  26.1 5.3 %collective-permute-start.12 = (bf16[16,1280]{1,0:T(8,128)(2,1)S(1)}, bf16[16,1280]{1,0:T(8,128)(2,1)S(1)}, u32[]{:S(2)}, u32[]{:S(2)}) collective-permute-start(bf16[16,1280]{1,0:T(8,128)(2,1)S(1)} %add_convert_fusion), channel_id=1, source_target_pairs={{0,9},{1,8},{2,11},{3,10},{4,13},{5,12},{6,15},{7,14},{8,1},{9,0},... | collective-permute-start | bytes 122888 | tf_op jit(solution)/shard_map/ppermute | solution.py:28
  26.1 5.3 %collective-permute-start.11 = (bf16[16,1280]{1,0:T(8,128)(2,1)S(1)}, bf16[16,1280]{1,0:T(8,128)(2,1)S(1)}, u32[]{:S(2)}, u32[]{:S(2)}) collective-permute-start(bf16[16,1280]{1,0:T(8,128)(2,1)S(1)} %add_convert_fusion), channel_id=1, source_target_pairs={{0,5},{1,4},{2,7},{3,6},{4,1},{5,0},{6,3},{7,2},{8,13},{9,12},{10,... | collective-permute-start | bytes 122888 | tf_op jit(solution)/shard_map/ppermute | solution.py:28
  28.1 3.3 %collective-permute-start.10 = (bf16[16,1280]{1,0:T(8,128)(2,1)S(1)}, bf16[16,1280]{1,0:T(8,128)(2,1)S(1)}, u32[]{:S(2)}, u32[]{:S(2)}) collective-permute-start(bf16[16,1280]{1,0:T(8,128)(2,1)S(1)} %add_convert_fusion), channel_id=1, source_target_pairs={{0,1},{1,0},{2,3},{3,2},{4,5},{5,4},{6,7},{7,6},{8,9},{9,8},{10,11... | collective-permute-start | bytes 122888 | tf_op jit(solution)/shard_map/ppermute | solution.py:28
  31.8 3.8 %collective-permute-start.16 = (bf16[64,384]{1,0:T(8,128)(2,1)S(1)}, bf16[64,384]{1,0:T(8,128)(2,1)S(1)}, u32[]{:S(2)}, u32[]{:S(2)}) collective-permute-start(bf16[64,384]{1,0:T(8,128)(2,1)S(1)} %product.3.refs_0_), channel_id=1, source_target_pairs={{0,3},{1,2},{2,1},{3,0},{4,7},{5,6},{6,5},{7,4},{8,11},{9,10},{10,... | collective-permute-start | bytes 147464 | tf_op jit(solution)/shard_map/ppermute | solution.py:17
  32.7 4.2 %collective-permute-start.15 = (bf16[64,384]{1,0:T(8,128)(2,1)S(1)}, bf16[64,384]{1,0:T(8,128)(2,1)S(1)}, u32[]{:S(2)}, u32[]{:S(2)}) collective-permute-start(bf16[64,384]{1,0:T(8,128)(2,1)S(1)} %product.3.refs_0_), channel_id=1, source_target_pairs={{0,2},{1,3},{2,0},{3,1},{4,6},{5,7},{6,4},{7,5},{8,10},{9,11},{10,... | collective-permute-start | bytes 147464 | tf_op jit(solution)/shard_map/ppermute | solution.py:17
  33.6 3.4 %collective-permute-start.14 = (bf16[64,384]{1,0:T(8,128)(2,1)S(1)}, bf16[64,384]{1,0:T(8,128)(2,1)S(1)}, u32[]{:S(2)}, u32[]{:S(2)}) collective-permute-start(bf16[64,384]{1,0:T(8,128)(2,1)S(1)} %product.3.refs_0_), channel_id=1, source_target_pairs={{0,1},{1,0},{2,3},{3,2},{4,5},{5,4},{6,7},{7,6},{8,9},{9,8},{10,11... | collective-permute-start | bytes 147464 | tf_op jit(solution)/shard_map/ppermute | solution.py:17
